TPU v7x, 32 devices: a whole 2x2x4 slice. The times are simulated.
32 devices in a mesh: mem: 8 (over y, x, core), reg: 4 (over z).
Axes of the slice: x: 2, y: 2, z: 4, core: 2. Of those that a mesh axis runs over, the one named last changes fastest.
Arguments:
- ens_state: bfloat16 [128, 16384], P('mem', 'reg'), may hold values from -6 to 6
- ens_obs: bfloat16 [128, 8192], P('mem', 'reg'), may hold values from -6 to 6
- innov: bfloat16 [128, 8192], P('mem', 'reg'), may hold values from -6 to 6
- state_coord: int32 [2, 16384], P(None, 'reg'), may hold values from 0 to 63
- obs_coord: int32 [2, 8192], replicated, may hold values from 0 to 63
- obs_routes: int32 [64, 1], replicated, may hold values from 0 to 3; in each aligned block of 16 rows (0 to 15, 16 to 31, ...) at most 8 rows name the same one
Outputs:
- analysis: bfloat16 [128, 16384], P('mem', 'reg')
Inputs may be any that keep to these rules, and one draw needn't show every extreme that they name: `obs_routes`: in each aligned block of 16 rows (the observation blocks of one source region) no region is named by more than 8 rows, a bound that some block reaches.
All inputs are finite; a program needn't handle non-finite values.
Results may differ from a plain program's by a relative error of at most 0.0022.
The roundings to bfloat16 on the way count: a program that leaves them out, or rounds other values in their place, can miss the bound.
Values may be sent and summed in bfloat16 or wider, within the bound.
No kernel may reach another device: no remote copies, remote signals or barrier semaphores. Data moves between devices by JAX's collectives and lax.ppermute only.
A program may use at most 64 MiB of HBM per device.

v0:
```python
import functools
import math

import jax
import jax.numpy as jnp
from jax import lax
from jax.experimental import pallas as pl
from jax.experimental.pallas import tpu as pltpu
from jax.sharding import PartitionSpec as P


BLK = 128
LOC = 32
SLOTS = 4


VMEM = pl.BlockSpec(memory_space=pltpu.VMEM)
SMEM = pl.BlockSpec(memory_space=pltpu.SMEM)
HBM = pl.BlockSpec(memory_space=pltpu.HBM)
PARAMS = pltpu.CompilerParams(vmem_limit_bytes=16 << 20)


def list_blocks(routes_ref, listed_ref, base, per_region, regions, capacity):
    unroll = math.gcd(per_region, 16)

    def clear(i, carry):
        listed_ref[i] = -1
        return carry

    lax.fori_loop(0, regions * capacity, clear, 0, unroll=unroll)

    def step(k, counts):
        r = routes_ref[base + k]
        c = counts[0]
        for i in range(1, regions):
            c = jnp.where(r == i, counts[i], c)
        listed_ref[r * capacity + c] = k
        return tuple(jnp.where(r == i, n + 1, n) for i, n in enumerate(counts))

    lax.fori_loop(0, per_region, step, (jnp.int32(0),) * regions, unroll=unroll)


def gather_kernel(dims, routes_hbm, obs_hbm, innov_hbm, *refs):
    regions, per_region, capacity = dims
    outs = refs[:regions]
    routes_ref, obs_ref, innov_ref, listed_ref, sems = refs[regions:]
    me = lax.axis_index("reg")
    loads = [
        pltpu.make_async_copy(src, dst, sems.at[i])
        for i, (src, dst) in enumerate(
            ((routes_hbm, routes_ref), (obs_hbm, obs_ref), (innov_hbm, innov_ref))
        )
    ]
    for load in loads:
        load.start()
    loads[0].wait()
    list_blocks(routes_ref, listed_ref, me * per_region, per_region, regions, capacity)
    loads[1].wait()
    loads[2].wait()
    for step, out_ref in enumerate(outs):
        target = lax.bitwise_xor(me, step)
        for c in range(capacity):
            k = listed_ref[target * capacity + c]
            columns = pl.ds(pl.multiple_of(jnp.maximum(k, 0) * BLK, BLK), BLK)
            for part, ref in enumerate((obs_ref, innov_ref)):
                block = ref[:, columns]
                at = (part * capacity + c) * BLK
                out_ref[:, at : at + BLK] = jnp.where(k >= 0, block, jnp.zeros_like(block))


def arrange_kernel(dims, *refs):
    regions, share, width = dims
    out_ref = refs[regions]
    me = lax.axis_index("reg")
    for step in range(regions):
        source = lax.bitwise_xor(me, step)
        for j in range(share):
            for part in range(2):
                at = (part * share + j) * width
                out_ref[source * share + j, :, part * width : (part + 1) * width] = refs[step][
                    :, at : at + width
                ]


def split_kernel(bands, state_ref, out_ref):
    width = out_ref.shape[2]
    for b in range(bands):
        out_ref[b] = state_ref[:, b * width : (b + 1) * width]


def taper_kernel(dims, routes_ref, rows_ref, obs_ref, out_ref, listed_ref):
    regions, per_region, capacity, share, scale = dims
    width = out_ref.shape[1]
    region, band = lax.axis_index("reg"), lax.axis_index("mem")
    source = band // share
    first = (band % share) * SLOTS
    base = source * per_region
    list_blocks(routes_ref, listed_ref, base, per_region, regions, capacity)
    rows_at = pl.ds(pl.multiple_of(band * width, BLK), width)
    rows = terms(rows_ref[:, rows_at], -2.0 / (LOC * LOC), 1.0 / (LOC * LOC), False)
    for s in range(SLOTS):
        k = jnp.maximum(listed_ref[region * capacity + first + s], 0)
        block = pl.ds(pl.multiple_of((base + k) * BLK, BLK), BLK)
        columns = terms(obs_ref[:, block], 1.0, 1.0, True)
        square = lax.dot_general(
            columns, rows, (((0,), (0,)), ((), ())), preferred_element_type=jnp.float32
        )
        inverse = lax.rsqrt(jnp.maximum(square, 1.0 / (LOC * LOC)))
        ratio = square * inverse
        inner = (((-0.25 * scale) * ratio + 0.5 * scale) * ratio + 0.625 * scale) * ratio
        inner = (inner - 5.0 / 3.0 * scale) * square + scale
        rest = jnp.maximum(2.0 - ratio, 0.0)
        rest = rest * rest
        outer = ((scale / 12.0) * ratio + scale / 6.0) * ratio - scale / 24.0
        outer = outer * (rest * rest) * inverse
        out_ref[s * BLK : (s + 1) * BLK, :] = jnp.where(ratio <= 1.0, inner, outer)


def terms(xy, cross, unit, left):
    norm = xy[0:1] * xy[0:1] + xy[1:2] * xy[1:2]
    high = lax.bitwise_and(norm, -256)
    low = lax.bitwise_and(norm, 255)
    ones = jnp.ones_like(norm)
    own, other = [high, low], [ones, ones]
    order = own + other if left else other + own
    body = jnp.concatenate([xy] + order + [jnp.zeros_like(xy)], axis=0).astype(jnp.float32)
    at = lax.broadcasted_iota(jnp.int32, body.shape, 0)
    return (body * jnp.where(at < 2, cross, unit)).astype(jnp.bfloat16)


def centered(values):
    wide = values.astype(jnp.float32)
    return (wide - jnp.mean(wide, axis=0, keepdims=True)).astype(jnp.bfloat16)


def update_kernel(state_ref, both_ref, taper_ref, out_ref):
    bands, mem_dev, width = state_ref.shape
    members = bands * mem_dev
    state_anom = centered(state_ref[...].reshape(members, width))
    obs_anom = centered(both_ref[:, :, :width].reshape(members, width))
    innov = both_ref[:, :, width:].reshape(members, width)
    cov = lax.dot_general(
        obs_anom, state_anom, (((0,), (0,)), ((), ())), preferred_element_type=jnp.float32
    )
    tiles = (cov * taper_ref[...]).astype(jnp.bfloat16)
    out = lax.dot_general(
        innov, tiles, (((1,), (0,)), ((), ())), preferred_element_type=jnp.float32
    )
    out_ref[...] = out.astype(jnp.bfloat16).reshape(bands, mem_dev, width)


def add_kernel(state_ref, inc_ref, out_ref):
    bands, _, width = inc_ref.shape
    for b in range(bands):
        cols = slice(b * width, (b + 1) * width)
        total = state_ref[:, cols].astype(jnp.float32) + inc_ref[b].astype(jnp.float32)
        out_ref[:, cols] = total.astype(jnp.bfloat16)


def call(kernel, shapes, in_specs, *args, scratch=()):
    outs = [jax.ShapeDtypeStruct(s, d) for s, d in shapes]
    single = len(outs) == 1
    return pl.pallas_call(
        kernel,
        out_shape=outs[0] if single else outs,
        in_specs=in_specs,
        out_specs=VMEM if single else [VMEM] * len(outs),
        scratch_shapes=list(scratch),
        compiler_params=PARAMS,
    )(*args)


def per_device(ens_state, ens_obs, innov, state_coord, obs_coord, obs_routes):
    regions = lax.axis_size("reg")
    bands = lax.axis_size("mem")
    mem_dev, columns = ens_state.shape
    members = mem_dev * bands
    per_region = ens_obs.shape[1] // BLK
    capacity = SLOTS * bands // regions
    share = bands // regions
    width = SLOTS * BLK
    band_rows = columns // bands
    bf16 = jnp.bfloat16
    routes = obs_routes.reshape(-1)
    listed = pltpu.SMEM((regions * capacity,), jnp.int32)

    picked = call(
        functools.partial(gather_kernel, (regions, per_region, capacity)),
        [((mem_dev, 2 * capacity * BLK), bf16)] * regions,
        [HBM] * 3,
        *(pltpu.with_memory_space_constraint(x, pltpu.HBM) for x in (routes, ens_obs, innov)),
        scratch=[
            pltpu.SMEM(routes.shape, jnp.int32),
            pltpu.VMEM(ens_obs.shape, bf16),
            pltpu.VMEM(innov.shape, bf16),
            listed,
            pltpu.SemaphoreType.DMA((3,)),
        ],
    )
    received = [picked[0]]
    for step in range(1, regions):
        pairs = [(i, i ^ step) for i in range(regions)]
        received.append(lax.ppermute(picked[step], "reg", pairs))
    state_split = call(
        functools.partial(split_kernel, bands),
        [((bands, mem_dev, band_rows), bf16)],
        [VMEM],
        ens_state,
    )
    state_rows = lax.all_to_all(state_split, "mem", split_axis=0, concat_axis=0, tiled=True)
    taper = call(
        functools.partial(
            taper_kernel, (regions, per_region, capacity, share, 1.0 / (members - 1))
        ),
        [((width, band_rows), jnp.float32)],
        [SMEM, VMEM, VMEM],
        routes,
        state_coord,
        obs_coord,
        scratch=[listed],
    )
    both = call(
        functools.partial(arrange_kernel, (regions, share, width)),
        [((bands, mem_dev, 2 * width), bf16)],
        [VMEM] * regions,
        *received,
    )
    both = lax.all_to_all(both, "mem", split_axis=0, concat_axis=0, tiled=True)
    increments = call(
        update_kernel, [((bands, mem_dev, band_rows), bf16)], [VMEM] * 3, state_rows, both, taper
    )
    returned = lax.all_to_all(increments, "mem", split_axis=0, concat_axis=0, tiled=True)
    return call(add_kernel, [((mem_dev, columns), bf16)], [VMEM] * 2, ens_state, returned)


def solution(mesh):
    return jax.shard_map(
        per_device,
        mesh=mesh,
        in_specs=(P("mem", "reg"), P("mem", "reg"), P("mem", "reg"), P(None, "reg"), P(), P()),
        out_specs=P("mem", "reg"),
        check_vma=False,
    )
```

profile of v0, /device:TPU:0, one launch (start us, length us, event | category | flops | bytes accessed | tf_op | source)
XLA Modules:
  0.0 39.4 jit_solution(4758418352265941030)
XLA Ops:
  0.0 0.0 copy-start
  0.0 0.9 %copy-done = bf16[16,4096]{1,0:T(8,128)(2,1)S(1)} copy-done((bf16[16,4096]{1,0:T(8,128)(2,1)S(1)}, bf16[16,4096]{1,0:T(8,128)(2,1)}, u32[]{:S(2)}) %copy-start) | copy-done | bytes 131096
  0.9 0.7 %shard_map.64 = bf16[8,16,512]{2,1,0:T(8,128)(2,1)} custom-call(bf16[16,4096]{1,0:T(8,128)(2,1)S(1)} %copy-done), custom_call_target="tpu_custom_call" | custom-call | tf_op jit(solution)/shard_map/pallas_call | solution.py:163
  1.6 5.2 %all-to-all-start = ((bf16[8,16,512]{2,1,0:T(8,128)(2,1)}), bf16[8,16,512]{2,1,0:T(8,128)(2,1)S(1)}, u32[]{:S(2)}, u32[]{:S(2)}) async-start(bf16[8,16,512]{2,1,0:T(8,128)(2,1)} %shard_map.64), calls=%async_computation | async-start | bytes 262144 | tf_op jit(solution)/shard_map/all_to_all | solution.py:210
  6.8 1.0 %shard_map.65 = (bf16[16,2048]{1,0:T(8,128)(2,1)S(1)}, bf16[16,2048]{1,0:T(8,128)(2,1)S(1)}, bf16[16,2048]{1,0:T(8,128)(2,1)S(1)}, bf16[16,2048]{1,0:T(8,128)(2,1)S(1)}) custom-call(s32[64]{0:T(128)} %bitcast.1, bf16[16,2048]{1,0:T(8,128)(2,1)} %obs_hbm.1, bf16[16,2048]{1,0:T(8,128)(2,1)} %innov_hbm.1), custom_call_target="tpu_custom_call" | custom-call | tf_op jit(solution)/shard_map/pallas_call | solution.py:163
  7.8 1.6 %collective-permute-start = (bf16[16,2048]{1,0:T(8,128)(2,1)S(1)}, bf16[16,2048]{1,0:T(8,128)(2,1)S(1)}, u32[]{:S(2)}, u32[]{:S(2)}) collective-permute-start(bf16[16,2048]{1,0:T(8,128)(2,1)S(1)} %get-tuple-element.10), channel_id=1, source_target_pairs={{0,1},{1,0},{2,3},{3,2},{4,5},{5,4},{6,7},{7,6},{8,9},{9,8},{10,11... | collective-permute-start | bytes 196616 | tf_op jit(solution)/shard_map/ppermute | solution.py:203
  9.4 2.6 %collective-permute-start.1 = (bf16[16,2048]{1,0:T(8,128)(2,1)S(1)}, bf16[16,2048]{1,0:T(8,128)(2,1)S(1)}, u32[]{:S(2)}, u32[]{:S(2)}) collective-permute-start(bf16[16,2048]{1,0:T(8,128)(2,1)S(1)} %get-tuple-element.11), channel_id=1, source_target_pairs={{0,2},{1,3},{2,0},{3,1},{4,6},{5,7},{6,4},{7,5},{8,10},{9,11},{10,... | collective-permute-start | bytes 196616 | tf_op jit(solution)/shard_map/ppermute | solution.py:203
  12.0 0.2 collective-permute-start.2
  12.2 0.1 collective-permute-done.refs_1_
  12.4 4.1 %collective-permute-done.1.refs_2_ = bf16[16,2048]{1,0:T(8,128)(2,1)S(1)} collective-permute-done((bf16[16,2048]{1,0:T(8,128)(2,1)S(1)}, bf16[16,2048]{1,0:T(8,128)(2,1)S(1)}, u32[]{:S(2)}, u32[]{:S(2)}) %collective-permute-start.1) | collective-permute-done | bytes 65568 | tf_op jit(solution)/shard_map/ppermute | solution.py:203
  16.4 1.7 %collective-permute-done.2.refs_3_ = bf16[16,2048]{1,0:T(8,128)(2,1)S(1)} collective-permute-done((bf16[16,2048]{1,0:T(8,128)(2,1)S(1)}, bf16[16,2048]{1,0:T(8,128)(2,1)S(1)}, u32[]{:S(2)}, u32[]{:S(2)}) %collective-permute-start.2) | collective-permute-done | bytes 65568 | tf_op jit(solution)/shard_map/ppermute | solution.py:203
  18.1 0.7 %shard_map.66 = bf16[8,16,1024]{2,1,0:T(8,128)(2,1)} custom-call(bf16[16,2048]{1,0:T(8,128)(2,1)S(1)} %get-tuple-element.9.refs_0_, bf16[16,2048]{1,0:T(8,128)(2,1)S(1)} %collective-permute-done.refs_1_, bf16[16,2048]{1,0:T(8,128)(2,1)S(1)} %collective-permute-done.1.refs_2_, bf16[16,2048]{1,0:T(8,128)(2,1)S(1)} %collective-permute-done.2.refs_3_), custom_call_target="tpu_custom_call" | custom-call | tf_op jit(solution)/shard_map/pallas_call | solution.py:163
  18.8 0.0 all-to-all-done.state_ref
  18.8 4.4 %all-to-all-start.1 = ((bf16[8,16,1024]{2,1,0:T(8,128)(2,1)}), bf16[8,16,1024]{2,1,0:T(8,128)(2,1)S(1)}, u32[]{:S(2)}, u32[]{:S(2)}) async-start(bf16[8,16,1024]{2,1,0:T(8,128)(2,1)} %shard_map.66), calls=%async_computation.1 | async-start | bytes 524288 | tf_op jit(solution)/shard_map/all_to_all | solution.py:228
  23.3 0.0 copy-done.2
  23.3 0.0 copy-done.3
  23.3 0.0 copy-done.4
  23.3 1.7 %shard_map.67.taper_ref = f32[512,512]{1,0:T(8,128)S(1)} custom-call(s32[64]{0:T(128)S(1)} %bitcast.2, s32[2,4096]{1,0:T(2,128)S(1)} %copy-done.3, s32[2,8192]{1,0:T(2,128)S(1)} %copy-done.2), custom_call_target="tpu_custom_call" | custom-call | tf_op jit(solution)/shard_map/pallas_call | solution.py:163
  25.0 5.2 %all-to-all-done.1.both_ref = bf16[8,16,1024]{2,1,0:T(8,128)(2,1)S(1)} async-done(((bf16[8,16,1024]{2,1,0:T(8,128)(2,1)}), bf16[8,16,1024]{2,1,0:T(8,128)(2,1)S(1)}, u32[]{:S(2)}, u32[]{:S(2)}) %all-to-all-start.1) | async-done | bytes 262176 | tf_op jit(solution)/shard_map/all_to_all | solution.py:228
  30.2 0.5 %shard_map.68 = bf16[8,16,512]{2,1,0:T(8,128)(2,1)S(1)} custom-call(bf16[8,16,512]{2,1,0:T(8,128)(2,1)S(1)} %all-to-all-done.state_ref, bf16[8,16,1024]{2,1,0:T(8,128)(2,1)S(1)} %all-to-all-done.1.both_ref, f32[512,512]{1,0:T(8,128)S(1)} %shard_map.67.taper_ref), custom_call_target="tpu_custom_call" | custom-call | tf_op jit(solution)/shard_map/pallas_call | solution.py:163
  30.7 0.0 copy-start.1
  30.7 8.0 %all_to_all.15.inc_ref = bf16[8,16,512]{2,1,0:T(8,128)(2,1)S(1)} all-to-all(bf16[8,16,512]{2,1,0:T(8,128)(2,1)S(1)} %shard_map.68), channel_id=1, replica_groups=mesh['mem'=8,'reg'=4] {'mem'}, dimensions={0} | all-to-all | bytes 262144 | tf_op jit(solution)/shard_map/all_to_all | solution.py:232
  38.8 0.0 copy-done.1
  38.8 0.7 %shard_map.69 = bf16[16,4096]{1,0:T(8,128)(2,1)} custom-call(bf16[16,4096]{1,0:T(8,128)(2,1)S(1)} %copy-done.1, bf16[8,16,512]{2,1,0:T(8,128)(2,1)S(1)} %all_to_all.15.inc_ref), custom_call_target="tpu_custom_call" | custom-call | tf_op jit(solution)/shard_map/pallas_call | solution.py:163
  (3 shorter events, 0.0 us)
Async XLA Ops:
  0.0 0.9 %copy-start = (bf16[16,4096]{1,0:T(8,128)(2,1)S(1)}, bf16[16,4096]{1,0:T(8,128)(2,1)}, u32[]{:S(2)}) copy-start(bf16[16,4096]{1,0:T(8,128)(2,1)} %state_ref.3) | copy-start | bytes 393220
  1.6 17.3 %all-to-all-start = ((bf16[8,16,512]{2,1,0:T(8,128)(2,1)}), bf16[8,16,512]{2,1,0:T(8,128)(2,1)S(1)}, u32[]{:S(2)}, u32[]{:S(2)}) async-start(bf16[8,16,512]{2,1,0:T(8,128)(2,1)} %shard_map.64), calls=%async_computation | async-start | bytes 262144 | tf_op jit(solution)/shard_map/all_to_all | solution.py:210
  7.8 4.6 %collective-permute-start = (bf16[16,2048]{1,0:T(8,128)(2,1)S(1)}, bf16[16,2048]{1,0:T(8,128)(2,1)S(1)}, u32[]{:S(2)}, u32[]{:S(2)}) collective-permute-start(bf16[16,2048]{1,0:T(8,128)(2,1)S(1)} %get-tuple-element.10), channel_id=1, source_target_pairs={{0,1},{1,0},{2,3},{3,2},{4,5},{5,4},{6,7},{7,6},{8,9},{9,8},{10,11... | collective-permute-start | bytes 196616 | tf_op jit(solution)/shard_map/ppermute | solution.py:203
  9.4 7.0 %collective-permute-start.1 = (bf16[16,2048]{1,0:T(8,128)(2,1)S(1)}, bf16[16,2048]{1,0:T(8,128)(2,1)S(1)}, u32[]{:S(2)}, u32[]{:S(2)}) collective-permute-start(bf16[16,2048]{1,0:T(8,128)(2,1)S(1)} %get-tuple-element.11), channel_id=1, source_target_pairs={{0,2},{1,3},{2,0},{3,1},{4,6},{5,7},{6,4},{7,5},{8,10},{9,11},{10,... | collective-permute-start | bytes 196616 | tf_op jit(solution)/shard_map/ppermute | solution.py:203
  12.0 6.1 %collective-permute-start.2 = (bf16[16,2048]{1,0:T(8,128)(2,1)S(1)}, bf16[16,2048]{1,0:T(8,128)(2,1)S(1)}, u32[]{:S(2)}, u32[]{:S(2)}) collective-permute-start(bf16[16,2048]{1,0:T(8,128)(2,1)S(1)} %get-tuple-element.12), channel_id=1, source_target_pairs={{0,3},{1,2},{2,1},{3,0},{4,7},{5,6},{6,5},{7,4},{8,11},{9,10},{10,... | collective-permute-start | bytes 196616 | tf_op jit(solution)/shard_map/ppermute | solution.py:203
  18.8 4.5 %copy-start.2 = (s32[2,8192]{1,0:T(2,128)S(1)}, s32[2,8192]{1,0:T(2,128)}, u32[]{:S(2)}) copy-start(s32[2,8192]{1,0:T(2,128)} %obs_ref.1) | copy-start | bytes 196612
  18.8 4.5 %copy-start.3 = (s32[2,4096]{1,0:T(2,128)S(1)}, s32[2,4096]{1,0:T(2,128)}, u32[]{:S(2)}) copy-start(s32[2,4096]{1,0:T(2,128)} %rows_ref.1) | copy-start | bytes 98308
  18.8 4.5 %copy-start.4 = (s32[64,1]{0,1:T(1,128)S(1)}, s32[64,1]{0,1:T(1,128)}, u32[]{:S(2)}) copy-start(s32[64,1]{0,1:T(1,128)} %param.11) | copy-start | bytes 772
  18.8 11.3 %all-to-all-start.1 = ((bf16[8,16,1024]{2,1,0:T(8,128)(2,1)}), bf16[8,16,1024]{2,1,0:T(8,128)(2,1)S(1)}, u32[]{:S(2)}, u32[]{:S(2)}) async-start(bf16[8,16,1024]{2,1,0:T(8,128)(2,1)} %shard_map.66), calls=%async_computation.1 | async-start | bytes 524288 | tf_op jit(solution)/shard_map/all_to_all | solution.py:228
  30.7 8.0 %copy-start.1 = (bf16[16,4096]{1,0:T(8,128)(2,1)S(1)}, bf16[16,4096]{1,0:T(8,128)(2,1)}, u32[]{:S(2)}) copy-start(bf16[16,4096]{1,0:T(8,128)(2,1)} %state_ref.3) | copy-start | bytes 393220
where the time goes:
time: 39.9 us; the launch traced here: 39.4 us
  starting transfers between devices  14.1 us (35%)
  waiting for transfers between devices  11 us (28%)
  blocking collectives  8.02 us (20%)
  Pallas kernels  5.31 us (13%)
  local copies, waits for them, and re-layouts  0.92 us (2%)
    all_to_all x1, blocking collectives, per_device(): lax.all_to_all(increments, 'mem', split_axis=0, concat_axis=0, tiled=True)  8.02 us
    ppermute x3, waiting for transfers between devices, per_device(): received.append(lax.ppermute(picked[step], 'reg', pairs))  5.84 us
    pallas_call x6, Pallas kernels, call(): pl.pallas_call(kernel, out_shape=outs[0] if single else outs, in_specs=in...  5.31 us
    all_to_all x1, starting transfers between devices, per_device(): lax.all_to_all(state_split, 'mem', split_axis=0, concat_axis=0, tiled=True)  5.2 us
    all_to_all x1, waiting for transfers between devices, per_device(): both = lax.all_to_all(both, 'mem', split_axis=0, concat_axis=0, tiled=True)  5.19 us
    ppermute x3, starting transfers between devices, per_device(): received.append(lax.ppermute(picked[step], 'reg', pairs))  4.45 us
    all_to_all x1, starting transfers between devices, per_device(): both = lax.all_to_all(both, 'mem', split_axis=0, concat_axis=0, tiled=True)  4.44 us
    unnamed x10, local copies, waits for them, and re-layouts  0.92 us
  transfers between devices with their start and end apart: 5, of which 4 were waited for; matrix products, arithmetic and copies ran while one was open for 0% of the time, Pallas kernels for 9%

commit v1 on v0

--- a/solution.py
+++ b/solution.py
@@ -68,24 +68,19 @@
                 out_ref[:, at : at + BLK] = jnp.where(k >= 0, block, jnp.zeros_like(block))
 
 
-def arrange_kernel(dims, *refs):
-    regions, share, width = dims
+def arrange_kernel(dims, state_ref, *refs):
+    regions, share, rows, width = dims
     out_ref = refs[regions]
     me = lax.axis_index("reg")
+    for b in range(regions * share):
+        out_ref[b, :, :rows] = state_ref[:, b * rows : (b + 1) * rows]
     for step in range(regions):
         source = lax.bitwise_xor(me, step)
         for j in range(share):
             for part in range(2):
                 at = (part * share + j) * width
-                out_ref[source * share + j, :, part * width : (part + 1) * width] = refs[step][
-                    :, at : at + width
-                ]
-
-
-def split_kernel(bands, state_ref, out_ref):
-    width = out_ref.shape[2]
-    for b in range(bands):
-        out_ref[b] = state_ref[:, b * width : (b + 1) * width]
+                to = rows + part * width
+                out_ref[source * share + j, :, to : to + width] = refs[step][:, at : at + width]
 
 
 def taper_kernel(dims, routes_ref, rows_ref, obs_ref, out_ref, listed_ref):
@@ -133,12 +128,13 @@
     return (wide - jnp.mean(wide, axis=0, keepdims=True)).astype(jnp.bfloat16)
 
 
-def update_kernel(state_ref, both_ref, taper_ref, out_ref):
-    bands, mem_dev, width = state_ref.shape
+def update_kernel(all_ref, taper_ref, out_ref):
+    bands, mem_dev, rows = out_ref.shape
     members = bands * mem_dev
-    state_anom = centered(state_ref[...].reshape(members, width))
-    obs_anom = centered(both_ref[:, :, :width].reshape(members, width))
-    innov = both_ref[:, :, width:].reshape(members, width)
+    width = taper_ref.shape[0]
+    state_anom = centered(all_ref[:, :, :rows].reshape(members, rows))
+    obs_anom = centered(all_ref[:, :, rows : rows + width].reshape(members, width))
+    innov = all_ref[:, :, rows + width :].reshape(members, width)
     cov = lax.dot_general(
         obs_anom, state_anom, (((0,), (0,)), ((), ())), preferred_element_type=jnp.float32
     )
@@ -146,7 +142,7 @@
     out = lax.dot_general(
         innov, tiles, (((1,), (0,)), ((), ())), preferred_element_type=jnp.float32
     )
-    out_ref[...] = out.astype(jnp.bfloat16).reshape(bands, mem_dev, width)
+    out_ref[...] = out.astype(jnp.bfloat16).reshape(bands, mem_dev, rows)
 
 
 def add_kernel(state_ref, inc_ref, out_ref):
@@ -201,13 +197,6 @@
     for step in range(1, regions):
         pairs = [(i, i ^ step) for i in range(regions)]
         received.append(lax.ppermute(picked[step], "reg", pairs))
-    state_split = call(
-        functools.partial(split_kernel, bands),
-        [((bands, mem_dev, band_rows), bf16)],
-        [VMEM],
-        ens_state,
-    )
-    state_rows = lax.all_to_all(state_split, "mem", split_axis=0, concat_axis=0, tiled=True)
     taper = call(
         functools.partial(
             taper_kernel, (regions, per_region, capacity, share, 1.0 / (members - 1))
@@ -219,15 +208,16 @@
         obs_coord,
         scratch=[listed],
     )
-    both = call(
-        functools.partial(arrange_kernel, (regions, share, width)),
-        [((bands, mem_dev, 2 * width), bf16)],
-        [VMEM] * regions,
+    sent = call(
+        functools.partial(arrange_kernel, (regions, share, band_rows, width)),
+        [((bands, mem_dev, band_rows + 2 * width), bf16)],
+        [VMEM] * (regions + 1),
+        ens_state,
         *received,
     )
-    both = lax.all_to_all(both, "mem", split_axis=0, concat_axis=0, tiled=True)
+    ensemble = lax.all_to_all(sent, "mem", split_axis=0, concat_axis=0, tiled=True)
     increments = call(
-        update_kernel, [((bands, mem_dev, band_rows), bf16)], [VMEM] * 3, state_rows, both, taper
+        update_kernel, [((bands, mem_dev, band_rows), bf16)], [VMEM] * 2, ensemble, taper
     )
     returned = lax.all_to_all(increments, "mem", split_axis=0, concat_axis=0, tiled=True)
     return call(add_kernel, [((mem_dev, columns), bf16)], [VMEM] * 2, ens_state, returned)

time: 39.9 us -> 35.2 us (0.88)
  starting transfers between devices: 14.1 us -> 9.56 us
  waiting for transfers between devices: 11 us -> 12.7 us
  local copies, waits for them, and re-layouts: 0.92 us -> 0.01 us
  Pallas kernels: 5.31 us -> 4.73 us
    all_to_all x2 -> x1, starting transfers between devices: 9.64 us -> 3.85 us  [per_device(): lax.all_to_all(sent, 'mem', split_axis=0, concat_axis=0, tiled=True)]
    all_to_all x2 -> x1, waiting for transfers between devices: 5.19 us -> 6.6 us  [per_device(): lax.all_to_all(sent, 'mem', split_axis=0, concat_axis=0, tiled=True)]
    ppermute x3, starting transfers between devices: 4.45 us -> 5.71 us  [per_device(): received.append(lax.ppermute(picked[step], 'reg', pairs))]
    unnamed x10 -> x8, local copies, waits for them, and re-layouts: 0.92 us -> 0.01 us
    pallas_call x6 -> x5, Pallas kernels: 5.31 us -> 4.73 us  [call(): pl.pallas_call(kernel, out_shape=outs[0] if single else outs, in_specs=in...]
  transfers between devices with their start and end apart: 5 -> 4, of which waited for: 4 -> 3; matrix products, arithmetic and copies ran while one was open for 0% -> 0% of each run, Pallas kernels for 9% -> 5%
where the time goes in v1:
time: 35.2 us; the launch traced here: 34.9 us
  waiting for transfers between devices  12.7 us (36%)
  starting transfers between devices  9.56 us (27%)
  blocking collectives  7.89 us (22%)
  Pallas kernels  4.73 us (13%)
    all_to_all x1, blocking collectives, per_device(): lax.all_to_all(increments, 'mem', split_axis=0, concat_axis=0, tiled=True)  7.89 us
    all_to_all x1, waiting for transfers between devices, per_device(): lax.all_to_all(sent, 'mem', split_axis=0, concat_axis=0, tiled=True)  6.6 us
    ppermute x3, waiting for transfers between devices, per_device(): received.append(lax.ppermute(picked[step], 'reg', pairs))  6.07 us
    ppermute x3, starting transfers between devices, per_device(): received.append(lax.ppermute(picked[step], 'reg', pairs))  5.71 us
    pallas_call x5, Pallas kernels, call(): pl.pallas_call(kernel, out_shape=outs[0] if single else outs, in_specs=in...  4.73 us
    all_to_all x1, starting transfers between devices, per_device(): lax.all_to_all(sent, 'mem', split_axis=0, concat_axis=0, tiled=True)  3.85 us
  transfers between devices with their start and end apart: 4, of which 3 were waited for; matrix products, arithmetic and copies ran while one was open for 0% of the time, Pallas kernels for 5%

profile of v1, /device:TPU:0, one launch (start us, length us, event | category | flops | bytes accessed | tf_op | source)
XLA Modules:
  0.0 34.9 jit_solution(2719029892172177685)
XLA Ops:
  0.0 0.0 copy-start
  0.0 1.1 %shard_map.64 = (bf16[16,2048]{1,0:T(8,128)(2,1)S(1)}, bf16[16,2048]{1,0:T(8,128)(2,1)S(1)}, bf16[16,2048]{1,0:T(8,128)(2,1)S(1)}, bf16[16,2048]{1,0:T(8,128)(2,1)S(1)}) custom-call(s32[64]{0:T(128)} %bitcast.1, bf16[16,2048]{1,0:T(8,128)(2,1)} %obs_hbm.1, bf16[16,2048]{1,0:T(8,128)(2,1)} %innov_hbm.1), custom_call_target="tpu_custom_call" | custom-call | tf_op jit(solution)/shard_map/pallas_call | solution.py:159
  1.1 3.1 %collective-permute-start = (bf16[16,2048]{1,0:T(8,128)(2,1)S(1)}, bf16[16,2048]{1,0:T(8,128)(2,1)S(1)}, u32[]{:S(2)}, u32[]{:S(2)}) collective-permute-start(bf16[16,2048]{1,0:T(8,128)(2,1)S(1)} %get-tuple-element.10), channel_id=1, source_target_pairs={{0,1},{1,0},{2,3},{3,2},{4,5},{5,4},{6,7},{7,6},{8,9},{9,8},{10,11... | collective-permute-start | bytes 196616 | tf_op jit(solution)/shard_map/ppermute | solution.py:199
  4.2 2.6 %collective-permute-start.1 = (bf16[16,2048]{1,0:T(8,128)(2,1)S(1)}, bf16[16,2048]{1,0:T(8,128)(2,1)S(1)}, u32[]{:S(2)}, u32[]{:S(2)}) collective-permute-start(bf16[16,2048]{1,0:T(8,128)(2,1)S(1)} %get-tuple-element.11), channel_id=1, source_target_pairs={{0,2},{1,3},{2,0},{3,1},{4,6},{5,7},{6,4},{7,5},{8,10},{9,11},{10,... | collective-permute-start | bytes 196616 | tf_op jit(solution)/shard_map/ppermute | solution.py:199
  6.8 0.0 collective-permute-start.2
  6.8 0.0 collective-permute-done.refs_1_
  6.8 4.7 %collective-permute-done.1.refs_2_ = bf16[16,2048]{1,0:T(8,128)(2,1)S(1)} collective-permute-done((bf16[16,2048]{1,0:T(8,128)(2,1)S(1)}, bf16[16,2048]{1,0:T(8,128)(2,1)S(1)}, u32[]{:S(2)}, u32[]{:S(2)}) %collective-permute-start.1) | collective-permute-done | bytes 65568 | tf_op jit(solution)/shard_map/ppermute | solution.py:199
  11.5 1.4 %collective-permute-done.2.refs_3_ = bf16[16,2048]{1,0:T(8,128)(2,1)S(1)} collective-permute-done((bf16[16,2048]{1,0:T(8,128)(2,1)S(1)}, bf16[16,2048]{1,0:T(8,128)(2,1)S(1)}, u32[]{:S(2)}, u32[]{:S(2)}) %collective-permute-start.2) | collective-permute-done | bytes 65568 | tf_op jit(solution)/shard_map/ppermute | solution.py:199
  12.9 0.0 copy-done
  12.9 0.8 %shard_map.65 = bf16[8,16,1536]{2,1,0:T(8,128)(2,1)} custom-call(bf16[16,4096]{1,0:T(8,128)(2,1)S(1)} %copy-done, bf16[16,2048]{1,0:T(8,128)(2,1)S(1)} %get-tuple-element.9.refs_0_, bf16[16,2048]{1,0:T(8,128)(2,1)S(1)} %collective-permute-done.refs_1_, bf16[16,2048]{1,0:T(8,128)(2,1)S(1)} %collective-permute-done.1.refs_2_, ...), custom_call_target="tpu_custom_call" | custom-call | tf_op jit(solution)/shard_map/pallas_call | solution.py:159
  13.6 0.0 copy-start.1
  13.6 0.0 copy-start.2
  13.6 0.0 copy-start.3
  13.6 3.9 %all-to-all-start = ((bf16[8,16,1536]{2,1,0:T(8,128)(2,1)}), bf16[8,16,1536]{2,1,0:T(8,128)(2,1)S(1)}, u32[]{:S(2)}, u32[]{:S(2)}) async-start(bf16[8,16,1536]{2,1,0:T(8,128)(2,1)} %shard_map.65), calls=%async_computation | async-start | bytes 786432 | tf_op jit(solution)/shard_map/all_to_all | solution.py:218
  17.5 0.0 copy-done.1
  17.5 0.0 copy-done.2
  17.5 0.0 copy-done.3
  17.5 1.7 %shard_map.66.taper_ref = f32[512,512]{1,0:T(8,128)S(1)} custom-call(s32[64]{0:T(128)S(1)} %bitcast.2, s32[2,4096]{1,0:T(2,128)S(1)} %copy-done.2, s32[2,8192]{1,0:T(2,128)S(1)} %copy-done.1), custom_call_target="tpu_custom_call" | custom-call | tf_op jit(solution)/shard_map/pallas_call | solution.py:159
  19.2 6.6 %all-to-all-done.all_ref = bf16[8,16,1536]{2,1,0:T(8,128)(2,1)S(1)} async-done(((bf16[8,16,1536]{2,1,0:T(8,128)(2,1)}), bf16[8,16,1536]{2,1,0:T(8,128)(2,1)S(1)}, u32[]{:S(2)}, u32[]{:S(2)}) %all-to-all-start) | async-done | bytes 393248 | tf_op jit(solution)/shard_map/all_to_all | solution.py:218
  25.8 0.5 %shard_map.67 = bf16[8,16,512]{2,1,0:T(8,128)(2,1)S(1)} custom-call(bf16[8,16,1536]{2,1,0:T(8,128)(2,1)S(1)} %all-to-all-done.all_ref, f32[512,512]{1,0:T(8,128)S(1)} %shard_map.66.taper_ref), custom_call_target="tpu_custom_call" | custom-call | tf_op jit(solution)/shard_map/pallas_call | solution.py:159
  26.3 7.9 %all_to_all.10.inc_ref = bf16[8,16,512]{2,1,0:T(8,128)(2,1)S(1)} all-to-all(bf16[8,16,512]{2,1,0:T(8,128)(2,1)S(1)} %shard_map.67), channel_id=1, replica_groups=mesh['mem'=8,'reg'=4] {'mem'}, dimensions={0} | all-to-all | bytes 262144 | tf_op jit(solution)/shard_map/all_to_all | solution.py:222
  34.2 0.7 %shard_map.68 = bf16[16,4096]{1,0:T(8,128)(2,1)} custom-call(bf16[16,4096]{1,0:T(8,128)(2,1)S(1)} %copy-done, bf16[8,16,512]{2,1,0:T(8,128)(2,1)S(1)} %all_to_all.10.inc_ref), custom_call_target="tpu_custom_call" | custom-call | tf_op jit(solution)/shard_map/pallas_call | solution.py:159
Async XLA Ops:
  0.0 12.9 %copy-start = (bf16[16,4096]{1,0:T(8,128)(2,1)S(1)}, bf16[16,4096]{1,0:T(8,128)(2,1)}, u32[]{:S(2)}) copy-start(bf16[16,4096]{1,0:T(8,128)(2,1)} %state_ref.3) | copy-start | bytes 393220
  1.1 5.7 %collective-permute-start = (bf16[16,2048]{1,0:T(8,128)(2,1)S(1)}, bf16[16,2048]{1,0:T(8,128)(2,1)S(1)}, u32[]{:S(2)}, u32[]{:S(2)}) collective-permute-start(bf16[16,2048]{1,0:T(8,128)(2,1)S(1)} %get-tuple-element.10), channel_id=1, source_target_pairs={{0,1},{1,0},{2,3},{3,2},{4,5},{5,4},{6,7},{7,6},{8,9},{9,8},{10,11... | collective-permute-start | bytes 196616 | tf_op jit(solution)/shard_map/ppermute | solution.py:199
  4.2 7.3 %collective-permute-start.1 = (bf16[16,2048]{1,0:T(8,128)(2,1)S(1)}, bf16[16,2048]{1,0:T(8,128)(2,1)S(1)}, u32[]{:S(2)}, u32[]{:S(2)}) collective-permute-start(bf16[16,2048]{1,0:T(8,128)(2,1)S(1)} %get-tuple-element.11), channel_id=1, source_target_pairs={{0,2},{1,3},{2,0},{3,1},{4,6},{5,7},{6,4},{7,5},{8,10},{9,11},{10,... | collective-permute-start | bytes 196616 | tf_op jit(solution)/shard_map/ppermute | solution.py:199
  6.8 6.1 %collective-permute-start.2 = (bf16[16,2048]{1,0:T(8,128)(2,1)S(1)}, bf16[16,2048]{1,0:T(8,128)(2,1)S(1)}, u32[]{:S(2)}, u32[]{:S(2)}) collective-permute-start(bf16[16,2048]{1,0:T(8,128)(2,1)S(1)} %get-tuple-element.12), channel_id=1, source_target_pairs={{0,3},{1,2},{2,1},{3,0},{4,7},{5,6},{6,5},{7,4},{8,11},{9,10},{10,... | collective-permute-start | bytes 196616 | tf_op jit(solution)/shard_map/ppermute | solution.py:199
  13.6 3.9 %copy-start.1 = (s32[2,8192]{1,0:T(2,128)S(1)}, s32[2,8192]{1,0:T(2,128)}, u32[]{:S(2)}) copy-start(s32[2,8192]{1,0:T(2,128)} %obs_ref.1) | copy-start | bytes 196612
  13.6 3.9 %copy-start.2 = (s32[2,4096]{1,0:T(2,128)S(1)}, s32[2,4096]{1,0:T(2,128)}, u32[]{:S(2)}) copy-start(s32[2,4096]{1,0:T(2,128)} %rows_ref.1) | copy-start | bytes 98308
  13.6 3.9 %copy-start.3 = (s32[64,1]{0,1:T(1,128)S(1)}, s32[64,1]{0,1:T(1,128)}, u32[]{:S(2)}) copy-start(s32[64,1]{0,1:T(1,128)} %param.11) | copy-start | bytes 772
  13.6 12.2 %all-to-all-start = ((bf16[8,16,1536]{2,1,0:T(8,128)(2,1)}), bf16[8,16,1536]{2,1,0:T(8,128)(2,1)S(1)}, u32[]{:S(2)}, u32[]{:S(2)}) async-start(bf16[8,16,1536]{2,1,0:T(8,128)(2,1)} %shard_map.65), calls=%async_computation | async-start | bytes 786432 | tf_op jit(solution)/shard_map/all_to_all | solution.py:218

commit v2 on v0

v2 whole, which is shorter than its diff:
```python
import functools
import math

import jax
import jax.numpy as jnp
from jax import lax
from jax.experimental import pallas as pl
from jax.experimental.pallas import tpu as pltpu
from jax.sharding import PartitionSpec as P


BLK = 128
LOC = 32
SLOTS = 4
CORES = 2


VMEM = pl.BlockSpec(memory_space=pltpu.VMEM)
SMEM = pl.BlockSpec(memory_space=pltpu.SMEM)
PARAMS = pltpu.CompilerParams(vmem_limit_bytes=16 << 20)


def list_blocks(routes_ref, listed_ref, base, per_region, regions, capacity):
    unroll = math.gcd(per_region, 16)

    def clear(i, carry):
        listed_ref[i] = -1
        return carry

    lax.fori_loop(0, regions * capacity, clear, 0, unroll=unroll)

    def step(k, counts):
        r = routes_ref[base + k]
        c = counts[0]
        for i in range(1, regions):
            c = jnp.where(r == i, counts[i], c)
        listed_ref[r * capacity + c] = k
        return tuple(jnp.where(r == i, n + 1, n) for i, n in enumerate(counts))

    lax.fori_loop(0, per_region, step, (jnp.int32(0),) * regions, unroll=unroll)


def load_kernel(*refs):
    half = len(refs) // 2
    sems = refs[-1]
    loads = [
        pltpu.make_async_copy(refs[i], refs[half + i], sems.at[i]) for i in range(half)
    ]
    for load in loads:
        load.start()
    for load in loads:
        load.wait()


def gather_kernel(dims, routes_ref, *refs):
    regions, per_region, capacity, share, chips = dims
    obs, innov, state = refs[0:2], refs[2:4], refs[4:6]
    routed, rows_out = refs[6 : 6 + regions], refs[6 + regions : 6 + regions + chips]
    listed_ref = refs[-1]
    members, rows = obs[0].shape[0], rows_out[0].shape[1]
    me, band = lax.axis_index("reg"), lax.axis_index("mem")
    chip, core = band // CORES, band % CORES
    list_blocks(routes_ref, listed_ref, me * per_region, per_region, regions, capacity)
    for step, out_ref in enumerate(routed):
        target = lax.bitwise_xor(me, step)
        for j in range(share // CORES):
            first = target * capacity + (j * CORES + core) * SLOTS
            for c in range(SLOTS):
                k = listed_ref[first + c]
                columns = pl.ds(pl.multiple_of(jnp.maximum(k, 0) * BLK, BLK), BLK)
                for part, pair in enumerate((obs, innov)):
                    at = ((j * 2 + part) * SLOTS + c) * BLK
                    for half, ref in enumerate(pair):
                        block = ref[:, columns]
                        block = jnp.where(k >= 0, block, jnp.zeros_like(block))
                        out_ref[half * members : (half + 1) * members, at : at + BLK] = block
    for step, out_ref in enumerate(rows_out):
        to = lax.bitwise_xor(chip, step) * CORES + core
        columns = pl.ds(pl.multiple_of(to * rows, BLK), rows)
        for half, ref in enumerate(state):
            out_ref[half * members : (half + 1) * members, :] = ref[:, columns]


def arrange_kernel(dims, *refs):
    regions, share = dims
    routed, outs = refs[:regions], refs[regions:]
    width = outs[0].shape[1]
    me, band = lax.axis_index("reg"), lax.axis_index("mem")
    chip, core = band // CORES, band % CORES
    for step, out_ref in enumerate(outs):
        to = lax.bitwise_xor(chip, step) * CORES + core
        held = lax.bitwise_xor(to // share, me)
        at = pl.multiple_of((to % share) // CORES * width, BLK)
        for t in range(regions):

            @pl.when(held == t)
            def _(ref=routed[t], out_ref=out_ref, at=at):
                out_ref[...] = ref[:, pl.ds(at, width)]


def taper_kernel(dims, routes_ref, rows_ref, obs_ref, out_ref, listed_ref):
    regions, per_region, capacity, share, scale = dims
    width = out_ref.shape[1]
    region, band = lax.axis_index("reg"), lax.axis_index("mem")
    source = band // share
    first = (band % share) * SLOTS
    base = source * per_region
    list_blocks(routes_ref, listed_ref, base, per_region, regions, capacity)
    rows_at = pl.ds(pl.multiple_of(band * width, BLK), width)
    rows = terms(rows_ref[:, rows_at], -2.0 / (LOC * LOC), 1.0 / (LOC * LOC), False)
    for s in range(SLOTS):
        k = jnp.maximum(listed_ref[region * capacity + first + s], 0)
        block = pl.ds(pl.multiple_of((base + k) * BLK, BLK), BLK)
        columns = terms(obs_ref[:, block], 1.0, 1.0, True)
        square = lax.dot_general(
            columns, rows, (((0,), (0,)), ((), ())), preferred_element_type=jnp.float32
        )
        inverse = lax.rsqrt(jnp.maximum(square, 1.0 / (LOC * LOC)))
        ratio = square * inverse
        inner = (((-0.25 * scale) * ratio + 0.5 * scale) * ratio + 0.625 * scale) * ratio
        inner = (inner - 5.0 / 3.0 * scale) * square + scale
        rest = jnp.maximum(2.0 - ratio, 0.0)
        rest = rest * rest
        outer = ((scale / 12.0) * ratio + scale / 6.0) * ratio - scale / 24.0
        outer = outer * (rest * rest) * inverse
        out_ref[s * BLK : (s + 1) * BLK, :] = jnp.where(ratio <= 1.0, inner, outer)


def terms(xy, cross, unit, left):
    norm = xy[0:1] * xy[0:1] + xy[1:2] * xy[1:2]
    high = lax.bitwise_and(norm, -256)
    low = lax.bitwise_and(norm, 255)
    ones = jnp.ones_like(norm)
    own, other = [high, low], [ones, ones]
    order = own + other if left else other + own
    body = jnp.concatenate([xy] + order + [jnp.zeros_like(xy)], axis=0).astype(jnp.float32)
    at = lax.broadcasted_iota(jnp.int32, body.shape, 0)
    return (body * jnp.where(at < 2, cross, unit)).astype(jnp.bfloat16)


def centered(values):
    wide = values.astype(jnp.float32)
    return (wide - jnp.mean(wide, axis=0, keepdims=True)).astype(jnp.bfloat16)


def update_kernel(chips, *refs):
    state, both = refs[:chips], refs[chips : 2 * chips]
    taper_ref, outs = refs[2 * chips], refs[2 * chips + 1 :]
    members, width = state[0].shape[0], taper_ref.shape[0]
    state_anom = centered(jnp.concatenate([ref[...] for ref in state], axis=0))
    obs_anom = centered(jnp.concatenate([ref[:, :width] for ref in both], axis=0))
    innov = jnp.concatenate([ref[:, width:] for ref in both], axis=0)
    cov = lax.dot_general(
        obs_anom, state_anom, (((0,), (0,)), ((), ())), preferred_element_type=jnp.float32
    )
    tiles = (cov * taper_ref[...]).astype(jnp.bfloat16)
    out = lax.dot_general(
        innov, tiles, (((1,), (0,)), ((), ())), preferred_element_type=jnp.float32
    ).astype(jnp.bfloat16)
    for k, out_ref in enumerate(outs):
        out_ref[...] = out[k * members : (k + 1) * members]


def swap_kernel(*refs):
    out_ref = refs[-1]
    members = out_ref.shape[1]
    for k, ref in enumerate(refs[:-1]):
        out_ref[k] = ref[members:, :]


def add_kernel(chips, state_ref, *refs):
    own, other_ref, out_ref = refs[:chips], refs[chips], refs[chips + 1]
    _, members, rows = other_ref.shape
    band = lax.axis_index("mem")
    chip, core = band // CORES, band % CORES
    for k in range(chips):
        first = lax.bitwise_xor(chip, k) * CORES
        for which, inc in ((core, own[k][:members, :]), (CORES - 1 - core, other_ref[k])):
            columns = pl.ds(pl.multiple_of((first + which) * rows, BLK), rows)
            total = state_ref[:, columns].astype(jnp.float32) + inc.astype(jnp.float32)
            out_ref[:, columns] = total.astype(jnp.bfloat16)


def call(kernel, shapes, in_specs, *args, scratch=()):
    outs = [jax.ShapeDtypeStruct(s, d) for s, d in shapes]
    single = len(outs) == 1
    result = pl.pallas_call(
        kernel,
        out_shape=outs[0] if single else outs,
        in_specs=in_specs,
        out_specs=VMEM if single else [VMEM] * len(outs),
        scratch_shapes=list(scratch),
        compiler_params=PARAMS,
    )(*args)
    return result if single else list(result)


def swap(value, axis, step):
    pairs = [(i, i ^ step) for i in range(lax.axis_size(axis))]
    return lax.ppermute(value, axis, pairs)


def per_device(ens_state, ens_obs, innov, state_coord, obs_coord, obs_routes):
    regions = lax.axis_size("reg")
    bands = lax.axis_size("mem")
    mem_dev, columns = ens_state.shape
    members = mem_dev * bands
    per_region = ens_obs.shape[1] // BLK
    capacity = SLOTS * bands // regions
    share = bands // regions
    chips = bands // CORES
    width = SLOTS * BLK
    rows = columns // bands
    held = CORES * mem_dev
    bf16 = jnp.bfloat16
    listed = pltpu.SMEM((regions * capacity,), jnp.int32)

    obs_other = swap(ens_obs, "mem", 1)
    innov_other = swap(innov, "mem", 1)
    state_other = swap(ens_state, "mem", 1)
    own = (ens_obs, innov, ens_state, obs_routes.reshape(-1))
    ens_obs, innov, ens_state, routes = call(
        load_kernel,
        [(x.shape, x.dtype) for x in own],
        [pl.BlockSpec(memory_space=pltpu.HBM)] * len(own),
        *(pltpu.with_memory_space_constraint(x, pltpu.HBM) for x in own),
        scratch=[pltpu.SemaphoreType.DMA((len(own),))],
    )
    picked = call(
        functools.partial(gather_kernel, (regions, per_region, capacity, share, chips)),
        [((held, share // CORES * 2 * width), bf16)] * regions + [((held, rows), bf16)] * chips,
        [SMEM] + [VMEM] * 6,
        routes,
        ens_obs,
        obs_other,
        innov,
        innov_other,
        ens_state,
        state_other,
        scratch=[listed],
    )
    routed, state = picked[:regions], picked[regions:]
    for step in range(1, regions):
        routed[step] = swap(routed[step], "reg", step)
    for k in range(1, chips):
        state[k] = swap(state[k], "mem", k * CORES)
    taper = call(
        functools.partial(
            taper_kernel, (regions, per_region, capacity, share, 1.0 / (members - 1))
        ),
        [((width, rows), jnp.float32)],
        [SMEM, VMEM, VMEM],
        routes,
        state_coord,
        obs_coord,
        scratch=[listed],
    )
    both = call(
        functools.partial(arrange_kernel, (regions, share)),
        [((held, 2 * width), bf16)] * chips,
        [VMEM] * regions,
        *routed,
    )
    for k in range(1, chips):
        both[k] = swap(both[k], "mem", k * CORES)
    increments = call(
        functools.partial(update_kernel, chips),
        [((held, rows), bf16)] * chips,
        [VMEM] * (2 * chips + 1),
        *state,
        *both,
        taper,
    )
    for k in range(1, chips):
        increments[k] = swap(increments[k], "mem", k * CORES)
    other = call(swap_kernel, [((chips, mem_dev, rows), bf16)], [VMEM] * chips, *increments)
    other = swap(other, "mem", 1)
    return call(
        functools.partial(add_kernel, chips),
        [((mem_dev, columns), bf16)],
        [VMEM] * (chips + 2),
        ens_state,
        *increments,
        other,
    )


def solution(mesh):
    return jax.shard_map(
        per_device,
        mesh=mesh,
        in_specs=(P("mem", "reg"), P("mem", "reg"), P("mem", "reg"), P(None, "reg"), P(), P()),
        out_specs=P("mem", "reg"),
        check_vma=False,
    )
```

time: 39.9 us -> 34.2 us (0.86)
  blocking collectives: 8.02 us -> 0 us
  starting transfers between devices: 14.1 us -> 18.3 us
  local copies, waits for them, and re-layouts: 0.92 us -> 0.01 us
  Pallas kernels: 5.31 us -> 4.83 us
    ppermute x3 -> x16, starting transfers between devices: 4.45 us -> 18.3 us  [swap(): return lax.ppermute(value, axis, pairs)]
    all_to_all x2 -> x0, starting transfers between devices: 9.64 us -> none  [the longest x1 5.2 us: per_device(): lax.all_to_all(state_split, 'mem', split_axis=0, concat_axis=0, tiled=True)]
    all_to_all x1 -> x0, blocking collectives: 8.02 us -> none  [per_device(): lax.all_to_all(increments, 'mem', split_axis=0, concat_axis=0, tiled=True)]
    all_to_all x2 -> x0, waiting for transfers between devices: 5.19 us -> none  [the longest x1 5.19 us: per_device(): both = lax.all_to_all(both, 'mem', split_axis=0, concat_axis=0, tiled=True)]
    ppermute x3 -> x16, waiting for transfers between devices: 5.84 us -> 10.8 us  [swap(): return lax.ppermute(value, axis, pairs)]
    unnamed x10 -> x4, local copies, waits for them, and re-layouts: 0.92 us -> 0.01 us
    pallas_call x6 -> x7, Pallas kernels: 5.31 us -> 4.83 us  [call(): pl.pallas_call(kernel, out_shape=outs[0] if single else outs, in_specs=in...]
  transfers between devices with their start and end apart: 5 -> 16, of which waited for: 4 -> 8; matrix products, arithmetic and copies ran while one was open for 0% -> 0% of each run, Pallas kernels for 9% -> 8%
where the time goes in v2:
time: 34.2 us; the launch traced here: 34.1 us
  starting transfers between devices  18.3 us (54%)
  waiting for transfers between devices  10.8 us (32%)
  Pallas kernels  4.83 us (14%)
    ppermute x16, starting transfers between devices, swap(): return lax.ppermute(value, axis, pairs)  18.3 us
    ppermute x16, waiting for transfers between devices, swap(): return lax.ppermute(value, axis, pairs)  10.8 us
    pallas_call x7, Pallas kernels, call(): pl.pallas_call(kernel, out_shape=outs[0] if single else outs, in_specs=in...  4.83 us
  transfers between devices with their start and end apart: 16, of which 8 were waited for; matrix products, arithmetic and copies ran while one was open for 0% of the time, Pallas kernels for 8%

profile of v2, /device:TPU:0, one launch (start us, length us, event | category | flops | bytes accessed | tf_op | source)
XLA Modules:
  0.0 34.1 jit_solution(4484043407223768976)
XLA Ops:
  0.0 0.5 %collective-permute-start.2 = (bf16[16,4096]{1,0:T(8,128)(2,1)}, bf16[16,4096]{1,0:T(8,128)(2,1)S(1)}, u32[]{:S(2)}, u32[]{:S(2)}) collective-permute-start(bf16[16,4096]{1,0:T(8,128)(2,1)} %refs_2_.1), channel_id=1, source_target_pairs={{0,4},{4,0},{8,12},{12,8},{16,20},{20,16},{24,28},{28,24},{1,5},{5... | collective-permute-start | bytes 393224 | tf_op jit(solution)/shard_map/ppermute | solution.py:200
  0.5 0.5 %collective-permute-start.1 = (bf16[16,2048]{1,0:T(8,128)(2,1)}, bf16[16,2048]{1,0:T(8,128)(2,1)S(1)}, u32[]{:S(2)}, u32[]{:S(2)}) collective-permute-start(bf16[16,2048]{1,0:T(8,128)(2,1)} %refs_1_.1), channel_id=1, source_target_pairs={{0,4},{4,0},{8,12},{12,8},{16,20},{20,16},{24,28},{28,24},{1,5},{5... | collective-permute-start | bytes 196616 | tf_op jit(solution)/shard_map/ppermute | solution.py:200
  1.0 1.0 %shard_map.64 = (bf16[16,2048]{1,0:T(8,128)(2,1)S(1)}, bf16[16,2048]{1,0:T(8,128)(2,1)S(1)}, bf16[16,4096]{1,0:T(8,128)(2,1)S(1)}, s32[64]{0:T(128)S(1)}) custom-call(bf16[16,2048]{1,0:T(8,128)(2,1)} %refs_0_.1, bf16[16,2048]{1,0:T(8,128)(2,1)} %refs_1_.1, bf16[16,4096]{1,0:T(8,128)(2,1)} %refs_2_.1, s32[64]{0:T(128)} %bitcast.1), custom_call_target="tpu_custom_call" | custom-call | tf_op jit(solution)/shard_map/pallas_call | solution.py:187
  2.1 0.8 %shard_map.65 = (bf16[32,1024]{1,0:T(8,128)(2,1)S(1)}, bf16[32,1024]{1,0:T(8,128)(2,1)S(1)}, bf16[32,1024]{1,0:T(8,128)(2,1)S(1)}, bf16[32,1024]{1,0:T(8,128)(2,...) custom-call(s32[64]{0:T(128)S(1)} %get-tuple-element.26.routes_ref, ...), custom_call_target="tpu_custom_call" | custom-call | tf_op jit(solution)/shard_map/pallas_call | solution.py:187
  2.9 3.0 %collective-permute-start.6 = (bf16[32,1024]{1,0:T(8,128)(2,1)S(1)}, bf16[32,1024]{1,0:T(8,128)(2,1)S(1)}, u32[]{:S(2)}, u32[]{:S(2)}) collective-permute-start(bf16[32,1024]{1,0:T(8,128)(2,1)S(1)} %get-tuple-element.34), channel_id=1, source_target_pairs={{0,1},{1,0},{2,3},{3,2},{4,5},{5,4},{6,7},{7,6},{8,9},{9,8},{10,11... | collective-permute-start | bytes 196616 | tf_op jit(solution)/shard_map/ppermute | solution.py:200
  5.9 2.6 %collective-permute-start.7 = (bf16[32,1024]{1,0:T(8,128)(2,1)S(1)}, bf16[32,1024]{1,0:T(8,128)(2,1)S(1)}, u32[]{:S(2)}, u32[]{:S(2)}) collective-permute-start(bf16[32,1024]{1,0:T(8,128)(2,1)S(1)} %get-tuple-element.35), channel_id=1, source_target_pairs={{0,2},{1,3},{2,0},{3,1},{4,6},{5,7},{6,4},{7,5},{8,10},{9,11},{10,... | collective-permute-start | bytes 196616 | tf_op jit(solution)/shard_map/ppermute | solution.py:200
  8.5 1.7 %collective-permute-start.3 = (bf16[32,512]{1,0:T(8,128)(2,1)S(1)}, bf16[32,512]{1,0:T(8,128)(2,1)S(1)}, u32[]{:S(2)}, u32[]{:S(2)}) collective-permute-start(bf16[32,512]{1,0:T(8,128)(2,1)S(1)} %get-tuple-element.30), channel_id=1, source_target_pairs={{0,8},{4,12},{8,0},{12,4},{16,24},{20,28},{24,16},{28,20},{1,9},{5... | collective-permute-start | bytes 98312 | tf_op jit(solution)/shard_map/ppermute | solution.py:200
  10.2 3.2 %collective-permute-done.7.refs_2_ = bf16[32,1024]{1,0:T(8,128)(2,1)S(1)} collective-permute-done((bf16[32,1024]{1,0:T(8,128)(2,1)S(1)}, bf16[32,1024]{1,0:T(8,128)(2,1)S(1)}, u32[]{:S(2)}, u32[]{:S(2)}) %collective-permute-start.7) | collective-permute-done | bytes 65568 | tf_op jit(solution)/shard_map/ppermute | solution.py:200
  13.4 1.2 %collective-permute-done.8.refs_3_ = bf16[32,1024]{1,0:T(8,128)(2,1)S(1)} collective-permute-done((bf16[32,1024]{1,0:T(8,128)(2,1)S(1)}, bf16[32,1024]{1,0:T(8,128)(2,1)S(1)}, u32[]{:S(2)}, u32[]{:S(2)}) %collective-permute-start.8) | collective-permute-done | bytes 65568 | tf_op jit(solution)/shard_map/ppermute | solution.py:200
  14.8 1.6 %collective-permute-start.9 = (bf16[32,1024]{1,0:T(8,128)(2,1)S(1)}, bf16[32,1024]{1,0:T(8,128)(2,1)S(1)}, u32[]{:S(2)}, u32[]{:S(2)}) collective-permute-start(bf16[32,1024]{1,0:T(8,128)(2,1)S(1)} %get-tuple-element.38), channel_id=1, source_target_pairs={{0,8},{4,12},{8,0},{12,4},{16,24},{20,28},{24,16},{28,20},{1,9},{5... | collective-permute-start | bytes 196616 | tf_op jit(solution)/shard_map/ppermute | solution.py:200
  16.3 1.5 %collective-permute-start.10 = (bf16[32,1024]{1,0:T(8,128)(2,1)S(1)}, bf16[32,1024]{1,0:T(8,128)(2,1)S(1)}, u32[]{:S(2)}, u32[]{:S(2)}) collective-permute-start(bf16[32,1024]{1,0:T(8,128)(2,1)S(1)} %get-tuple-element.39), channel_id=1, source_target_pairs={{0,16},{4,20},{8,24},{12,28},{16,0},{20,4},{24,8},{28,12},{1,17},{... | collective-permute-start | bytes 196616 | tf_op jit(solution)/shard_map/ppermute | solution.py:200
  17.9 0.5 %collective-permute-start.11 = (bf16[32,1024]{1,0:T(8,128)(2,1)S(1)}, bf16[32,1024]{1,0:T(8,128)(2,1)S(1)}, u32[]{:S(2)}, u32[]{:S(2)}) collective-permute-start(bf16[32,1024]{1,0:T(8,128)(2,1)S(1)} %get-tuple-element.40), channel_id=1, source_target_pairs={{0,24},{4,28},{8,16},{12,20},{16,8},{20,12},{24,0},{28,4},{1,25},{... | collective-permute-start | bytes 196616 | tf_op jit(solution)/shard_map/ppermute | solution.py:200
  18.3 1.5 %collective-permute-start.4 = (bf16[32,512]{1,0:T(8,128)(2,1)S(1)}, bf16[32,512]{1,0:T(8,128)(2,1)S(1)}, u32[]{:S(2)}, u32[]{:S(2)}) collective-permute-start(bf16[32,512]{1,0:T(8,128)(2,1)S(1)} %get-tuple-element.31), channel_id=1, source_target_pairs={{0,16},{4,20},{8,24},{12,28},{16,0},{20,4},{24,8},{28,12},{1,17},{... | collective-permute-start | bytes 98312 | tf_op jit(solution)/shard_map/ppermute | solution.py:200
  19.9 1.4 %collective-permute-start.5 = (bf16[32,512]{1,0:T(8,128)(2,1)S(1)}, bf16[32,512]{1,0:T(8,128)(2,1)S(1)}, u32[]{:S(2)}, u32[]{:S(2)}) collective-permute-start(bf16[32,512]{1,0:T(8,128)(2,1)S(1)} %get-tuple-element.32), channel_id=1, source_target_pairs={{0,24},{4,28},{8,16},{12,20},{16,8},{20,12},{24,0},{28,4},{1,25},{... | collective-permute-start | bytes 98312 | tf_op jit(solution)/shard_map/ppermute | solution.py:200
  21.3 1.7 %shard_map.67.refs_8_ = f32[512,512]{1,0:T(8,128)S(1)} custom-call(s32[64]{0:T(128)S(1)} %get-tuple-element.26.routes_ref, s32[2,4096]{1,0:T(2,128)S(1)} %copy-done.1, s32[2,8192]{1,0:T(2,128)S(1)} %copy-done), custom_call_target="tpu_custom_call" | custom-call | tf_op jit(solution)/shard_map/pallas_call | solution.py:187
  23.0 1.9 %collective-permute-done.5.refs_3_ = bf16[32,512]{1,0:T(8,128)(2,1)S(1)} collective-permute-done((bf16[32,512]{1,0:T(8,128)(2,1)S(1)}, bf16[32,512]{1,0:T(8,128)(2,1)S(1)}, u32[]{:S(2)}, u32[]{:S(2)}) %collective-permute-start.5) | collective-permute-done | bytes 32800 | tf_op jit(solution)/shard_map/ppermute | solution.py:200
  24.9 0.5 %shard_map.68 = (bf16[32,512]{1,0:T(8,128)(2,1)S(1)}, bf16[32,512]{1,0:T(8,128)(2,1)S(1)}, bf16[32,512]{1,0:T(8,128)(2,1)S(1)}, bf16[32,512]{1,0:T(8,128)(2,1)S(1)}) custom-call(bf16[32,512]{1,0:T(8,128)(2,1)S(1)} %get-tuple-element.29.refs_0_, bf16[32,512]{1,0:T(8,128)(2,1)S(1)} %collective-permute-done.3.refs_1_, ...), custom_call_target="tpu_custom_call" | custom-call | tf_op jit(solution)/shard_map/pallas_call | solution.py:187
  25.5 1.4 %collective-permute-start.12 = (bf16[32,512]{1,0:T(8,128)(2,1)S(1)}, bf16[32,512]{1,0:T(8,128)(2,1)S(1)}, u32[]{:S(2)}, u32[]{:S(2)}) collective-permute-start(bf16[32,512]{1,0:T(8,128)(2,1)S(1)} %get-tuple-element.42), channel_id=1, source_target_pairs={{0,8},{4,12},{8,0},{12,4},{16,24},{20,28},{24,16},{28,20},{1,9},{5... | collective-permute-start | bytes 98312 | tf_op jit(solution)/shard_map/ppermute | solution.py:200
  26.8 0.5 %collective-permute-start.13 = (bf16[32,512]{1,0:T(8,128)(2,1)S(1)}, bf16[32,512]{1,0:T(8,128)(2,1)S(1)}, u32[]{:S(2)}, u32[]{:S(2)}) collective-permute-start(bf16[32,512]{1,0:T(8,128)(2,1)S(1)} %get-tuple-element.43), channel_id=1, source_target_pairs={{0,16},{4,20},{8,24},{12,28},{16,0},{20,4},{24,8},{28,12},{1,17},{... | collective-permute-start | bytes 98312 | tf_op jit(solution)/shard_map/ppermute | solution.py:200
  27.3 1.7 %collective-permute-start.14 = (bf16[32,512]{1,0:T(8,128)(2,1)S(1)}, bf16[32,512]{1,0:T(8,128)(2,1)S(1)}, u32[]{:S(2)}, u32[]{:S(2)}) collective-permute-start(bf16[32,512]{1,0:T(8,128)(2,1)S(1)} %get-tuple-element.44), channel_id=1, source_target_pairs={{0,24},{4,28},{8,16},{12,20},{16,8},{20,12},{24,0},{28,4},{1,25},{... | collective-permute-start | bytes 98312 | tf_op jit(solution)/shard_map/ppermute | solution.py:200
  29.5 1.3 %collective-permute-done.13.refs_2_ = bf16[32,512]{1,0:T(8,128)(2,1)S(1)} collective-permute-done((bf16[32,512]{1,0:T(8,128)(2,1)S(1)}, bf16[32,512]{1,0:T(8,128)(2,1)S(1)}, u32[]{:S(2)}, u32[]{:S(2)}) %collective-permute-start.13) | collective-permute-done | bytes 32800 | tf_op jit(solution)/shard_map/ppermute | solution.py:200
  30.8 1.4 %collective-permute-done.14.refs_3_ = bf16[32,512]{1,0:T(8,128)(2,1)S(1)} collective-permute-done((bf16[32,512]{1,0:T(8,128)(2,1)S(1)}, bf16[32,512]{1,0:T(8,128)(2,1)S(1)}, u32[]{:S(2)}, u32[]{:S(2)}) %collective-permute-start.14) | collective-permute-done | bytes 32800 | tf_op jit(solution)/shard_map/ppermute | solution.py:200
  32.1 1.2 %collective-permute-done.15.refs_4_ = bf16[4,16,512]{2,1,0:T(8,128)(2,1)S(1)} collective-permute-done((bf16[4,16,512]{2,1,0:T(8,128)(2,1)S(1)}, bf16[4,16,512]{2,1,0:T(8,128)(2,1)S(1)}, u32[]{:S(2)}, u32[]{:S(2)}) %collective-permute-start.15) | collective-permute-done | bytes 65568 | tf_op jit(solution)/shard_map/ppermute | solution.py:200
  33.4 0.7 %shard_map.70 = bf16[16,4096]{1,0:T(8,128)(2,1)} custom-call(bf16[16,4096]{1,0:T(8,128)(2,1)S(1)} %get-tuple-element.25.refs_4_.state_ref, bf16[32,512]{1,0:T(8,128)(2,1)S(1)} %get-tuple-element.41.refs_0_, bf16[32,512]{1,0:T(8,128)(2,1)S(1)} %collective-permute-done.12.refs_1_, bf16[32,512]{1,0:T(8,128)(2,1)S(1)} %collective-permute-done.13.refs_2_, ...), custom_call_target="tpu_custom_call" | custom-call | tf_op jit(solution)/shard_map/pallas_call | solution.py:187
  (19 shorter events, 0.7 us)
Async XLA Ops:
  0.0 2.1 %collective-permute-start.2 = (bf16[16,4096]{1,0:T(8,128)(2,1)}, bf16[16,4096]{1,0:T(8,128)(2,1)S(1)}, u32[]{:S(2)}, u32[]{:S(2)}) collective-permute-start(bf16[16,4096]{1,0:T(8,128)(2,1)} %refs_2_.1), channel_id=1, source_target_pairs={{0,4},{4,0},{8,12},{12,8},{16,20},{20,16},{24,28},{28,24},{1,5},{5... | collective-permute-start | bytes 393224 | tf_op jit(solution)/shard_map/ppermute | solution.py:200
  0.5 1.5 %collective-permute-start = (bf16[16,2048]{1,0:T(8,128)(2,1)}, bf16[16,2048]{1,0:T(8,128)(2,1)S(1)}, u32[]{:S(2)}, u32[]{:S(2)}) collective-permute-start(bf16[16,2048]{1,0:T(8,128)(2,1)} %refs_0_.1), channel_id=1, source_target_pairs={{0,4},{4,0},{8,12},{12,8},{16,20},{20,16},{24,28},{28,24},{1,5},{5... | collective-permute-start | bytes 196616 | tf_op jit(solution)/shard_map/ppermute | solution.py:200
  0.5 1.6 %collective-permute-start.1 = (bf16[16,2048]{1,0:T(8,128)(2,1)}, bf16[16,2048]{1,0:T(8,128)(2,1)S(1)}, u32[]{:S(2)}, u32[]{:S(2)}) collective-permute-start(bf16[16,2048]{1,0:T(8,128)(2,1)} %refs_1_.1), channel_id=1, source_target_pairs={{0,4},{4,0},{8,12},{12,8},{16,20},{20,16},{24,28},{28,24},{1,5},{5... | collective-permute-start | bytes 196616 | tf_op jit(solution)/shard_map/ppermute | solution.py:200
  2.9 7.3 %collective-permute-start.6 = (bf16[32,1024]{1,0:T(8,128)(2,1)S(1)}, bf16[32,1024]{1,0:T(8,128)(2,1)S(1)}, u32[]{:S(2)}, u32[]{:S(2)}) collective-permute-start(bf16[32,1024]{1,0:T(8,128)(2,1)S(1)} %get-tuple-element.34), channel_id=1, source_target_pairs={{0,1},{1,0},{2,3},{3,2},{4,5},{5,4},{6,7},{7,6},{8,9},{9,8},{10,11... | collective-permute-start | bytes 196616 | tf_op jit(solution)/shard_map/ppermute | solution.py:200
  5.9 7.5 %collective-permute-start.7 = (bf16[32,1024]{1,0:T(8,128)(2,1)S(1)}, bf16[32,1024]{1,0:T(8,128)(2,1)S(1)}, u32[]{:S(2)}, u32[]{:S(2)}) collective-permute-start(bf16[32,1024]{1,0:T(8,128)(2,1)S(1)} %get-tuple-element.35), channel_id=1, source_target_pairs={{0,2},{1,3},{2,0},{3,1},{4,6},{5,7},{6,4},{7,5},{8,10},{9,11},{10,... | collective-permute-start | bytes 196616 | tf_op jit(solution)/shard_map/ppermute | solution.py:200
  8.5 6.2 %collective-permute-start.8 = (bf16[32,1024]{1,0:T(8,128)(2,1)S(1)}, bf16[32,1024]{1,0:T(8,128)(2,1)S(1)}, u32[]{:S(2)}, u32[]{:S(2)}) collective-permute-start(bf16[32,1024]{1,0:T(8,128)(2,1)S(1)} %get-tuple-element.36), channel_id=1, source_target_pairs={{0,3},{1,2},{2,1},{3,0},{4,7},{5,6},{6,5},{7,4},{8,11},{9,10},{10,... | collective-permute-start | bytes 196616 | tf_op jit(solution)/shard_map/ppermute | solution.py:200
  8.5 11.4 %collective-permute-start.3 = (bf16[32,512]{1,0:T(8,128)(2,1)S(1)}, bf16[32,512]{1,0:T(8,128)(2,1)S(1)}, u32[]{:S(2)}, u32[]{:S(2)}) collective-permute-start(bf16[32,512]{1,0:T(8,128)(2,1)S(1)} %get-tuple-element.30), channel_id=1, source_target_pairs={{0,8},{4,12},{8,0},{12,4},{16,24},{20,28},{24,16},{28,20},{1,9},{5... | collective-permute-start | bytes 98312 | tf_op jit(solution)/shard_map/ppermute | solution.py:200
  14.7 6.6 %copy-start = (s32[2,8192]{1,0:T(2,128)S(1)}, s32[2,8192]{1,0:T(2,128)}, u32[]{:S(2)}) copy-start(s32[2,8192]{1,0:T(2,128)} %obs_ref.1) | copy-start | bytes 196612
  14.7 6.6 %copy-start.1 = (s32[2,4096]{1,0:T(2,128)S(1)}, s32[2,4096]{1,0:T(2,128)}, u32[]{:S(2)}) copy-start(s32[2,4096]{1,0:T(2,128)} %rows_ref.1) | copy-start | bytes 98308
  14.8 10.1 %collective-permute-start.9 = (bf16[32,1024]{1,0:T(8,128)(2,1)S(1)}, bf16[32,1024]{1,0:T(8,128)(2,1)S(1)}, u32[]{:S(2)}, u32[]{:S(2)}) collective-permute-start(bf16[32,1024]{1,0:T(8,128)(2,1)S(1)} %get-tuple-element.38), channel_id=1, source_target_pairs={{0,8},{4,12},{8,0},{12,4},{16,24},{20,28},{24,16},{28,20},{1,9},{5... | collective-permute-start | bytes 196616 | tf_op jit(solution)/shard_map/ppermute | solution.py:200
  16.3 8.6 %collective-permute-start.10 = (bf16[32,1024]{1,0:T(8,128)(2,1)S(1)}, bf16[32,1024]{1,0:T(8,128)(2,1)S(1)}, u32[]{:S(2)}, u32[]{:S(2)}) collective-permute-start(bf16[32,1024]{1,0:T(8,128)(2,1)S(1)} %get-tuple-element.39), channel_id=1, source_target_pairs={{0,16},{4,20},{8,24},{12,28},{16,0},{20,4},{24,8},{28,12},{1,17},{... | collective-permute-start | bytes 196616 | tf_op jit(solution)/shard_map/ppermute | solution.py:200
  17.9 7.1 %collective-permute-start.11 = (bf16[32,1024]{1,0:T(8,128)(2,1)S(1)}, bf16[32,1024]{1,0:T(8,128)(2,1)S(1)}, u32[]{:S(2)}, u32[]{:S(2)}) collective-permute-start(bf16[32,1024]{1,0:T(8,128)(2,1)S(1)} %get-tuple-element.40), channel_id=1, source_target_pairs={{0,24},{4,28},{8,16},{12,20},{16,8},{20,12},{24,0},{28,4},{1,25},{... | collective-permute-start | bytes 196616 | tf_op jit(solution)/shard_map/ppermute | solution.py:200
  18.3 4.6 %collective-permute-start.4 = (bf16[32,512]{1,0:T(8,128)(2,1)S(1)}, bf16[32,512]{1,0:T(8,128)(2,1)S(1)}, u32[]{:S(2)}, u32[]{:S(2)}) collective-permute-start(bf16[32,512]{1,0:T(8,128)(2,1)S(1)} %get-tuple-element.31), channel_id=1, source_target_pairs={{0,16},{4,20},{8,24},{12,28},{16,0},{20,4},{24,8},{28,12},{1,17},{... | collective-permute-start | bytes 98312 | tf_op jit(solution)/shard_map/ppermute | solution.py:200
  19.9 5.1 %collective-permute-start.5 = (bf16[32,512]{1,0:T(8,128)(2,1)S(1)}, bf16[32,512]{1,0:T(8,128)(2,1)S(1)}, u32[]{:S(2)}, u32[]{:S(2)}) collective-permute-start(bf16[32,512]{1,0:T(8,128)(2,1)S(1)} %get-tuple-element.32), channel_id=1, source_target_pairs={{0,24},{4,28},{8,16},{12,20},{16,8},{20,12},{24,0},{28,4},{1,25},{... | collective-permute-start | bytes 98312 | tf_op jit(solution)/shard_map/ppermute | solution.py:200
  25.5 4.0 %collective-permute-start.12 = (bf16[32,512]{1,0:T(8,128)(2,1)S(1)}, bf16[32,512]{1,0:T(8,128)(2,1)S(1)}, u32[]{:S(2)}, u32[]{:S(2)}) collective-permute-start(bf16[32,512]{1,0:T(8,128)(2,1)S(1)} %get-tuple-element.42), channel_id=1, source_target_pairs={{0,8},{4,12},{8,0},{12,4},{16,24},{20,28},{24,16},{28,20},{1,9},{5... | collective-permute-start | bytes 98312 | tf_op jit(solution)/shard_map/ppermute | solution.py:200
  26.8 3.9 %collective-permute-start.13 = (bf16[32,512]{1,0:T(8,128)(2,1)S(1)}, bf16[32,512]{1,0:T(8,128)(2,1)S(1)}, u32[]{:S(2)}, u32[]{:S(2)}) collective-permute-start(bf16[32,512]{1,0:T(8,128)(2,1)S(1)} %get-tuple-element.43), channel_id=1, source_target_pairs={{0,16},{4,20},{8,24},{12,28},{16,0},{20,4},{24,8},{28,12},{1,17},{... | collective-permute-start | bytes 98312 | tf_op jit(solution)/shard_map/ppermute | solution.py:200
  27.3 4.8 %collective-permute-start.14 = (bf16[32,512]{1,0:T(8,128)(2,1)S(1)}, bf16[32,512]{1,0:T(8,128)(2,1)S(1)}, u32[]{:S(2)}, u32[]{:S(2)}) collective-permute-start(bf16[32,512]{1,0:T(8,128)(2,1)S(1)} %get-tuple-element.44), channel_id=1, source_target_pairs={{0,24},{4,28},{8,16},{12,20},{16,8},{20,12},{24,0},{28,4},{1,25},{... | collective-permute-start | bytes 98312 | tf_op jit(solution)/shard_map/ppermute | solution.py:200
  32.1 1.3 %collective-permute-start.15 = (bf16[4,16,512]{2,1,0:T(8,128)(2,1)S(1)}, bf16[4,16,512]{2,1,0:T(8,128)(2,1)S(1)}, u32[]{:S(2)}, u32[]{:S(2)}) collective-permute-start(bf16[4,16,512]{2,1,0:T(8,128)(2,1)S(1)} %shard_map.69), channel_id=1, source_target_pairs={{0,4},{4,0},{8,12},{12,8},{16,20},{20,16},{24,28},{28,24},{1,5},{5... | collective-permute-start | bytes 196616 | tf_op jit(solution)/shard_map/ppermute | solution.py:200

commit v3 on v2

--- a/solution.py
+++ b/solution.py
@@ -62,9 +62,12 @@
     chip, core = band // CORES, band % CORES
     list_blocks(routes_ref, listed_ref, me * per_region, per_region, regions, capacity)
     for step, out_ref in enumerate(routed):
+        hop = int(step != 0)
         target = lax.bitwise_xor(me, step)
         for j in range(share // CORES):
-            first = target * capacity + (j * CORES + core) * SLOTS
+            to = me * (share // CORES) + j
+            parity = jnp.where(to == chip, lax.bitwise_xor(core, hop), lax.bitwise_xor(core, 1 - hop))
+            first = target * capacity + (j * CORES + parity) * SLOTS
             for c in range(SLOTS):
                 k = listed_ref[first + c]
                 columns = pl.ds(pl.multiple_of(jnp.maximum(k, 0) * BLK, BLK), BLK)
@@ -73,9 +76,11 @@
                     for half, ref in enumerate(pair):
                         block = ref[:, columns]
                         block = jnp.where(k >= 0, block, jnp.zeros_like(block))
-                        out_ref[half * members : (half + 1) * members, at : at + BLK] = block
+                        row = (half ^ hop) * members
+                        out_ref[row : row + members, at : at + BLK] = block
     for step, out_ref in enumerate(rows_out):
-        to = lax.bitwise_xor(chip, step) * CORES + core
+        parity = lax.bitwise_xor(core, int(step != 0))
+        to = lax.bitwise_xor(chip, step) * CORES + parity
         columns = pl.ds(pl.multiple_of(to * rows, BLK), rows)
         for half, ref in enumerate(state):
             out_ref[half * members : (half + 1) * members, :] = ref[:, columns]
@@ -85,12 +90,11 @@
     regions, share = dims
     routed, outs = refs[:regions], refs[regions:]
     width = outs[0].shape[1]
-    me, band = lax.axis_index("reg"), lax.axis_index("mem")
-    chip, core = band // CORES, band % CORES
+    me, chip = lax.axis_index("reg"), lax.axis_index("mem") // CORES
     for step, out_ref in enumerate(outs):
-        to = lax.bitwise_xor(chip, step) * CORES + core
-        held = lax.bitwise_xor(to // share, me)
-        at = pl.multiple_of((to % share) // CORES * width, BLK)
+        to = lax.bitwise_xor(chip, step)
+        held = lax.bitwise_xor(to // (share // CORES), me)
+        at = pl.multiple_of(to % (share // CORES) * width, BLK)
         for t in range(regions):
 
             @pl.when(held == t)
@@ -175,7 +179,8 @@
     chip, core = band // CORES, band % CORES
     for k in range(chips):
         first = lax.bitwise_xor(chip, k) * CORES
-        for which, inc in ((core, own[k][:members, :]), (CORES - 1 - core, other_ref[k])):
+        parity = lax.bitwise_xor(core, int(k != 0))
+        for which, inc in ((parity, own[k][:members, :]), (1 - parity, other_ref[k])):
             columns = pl.ds(pl.multiple_of((first + which) * rows, BLK), rows)
             total = state_ref[:, columns].astype(jnp.float32) + inc.astype(jnp.float32)
             out_ref[:, columns] = total.astype(jnp.bfloat16)
@@ -195,9 +200,11 @@
     return result if single else list(result)
 
 
-def swap(value, axis, step):
-    pairs = [(i, i ^ step) for i in range(lax.axis_size(axis))]
-    return lax.ppermute(value, axis, pairs)
+def swap(value, mem=0, reg=0):
+    bands, regions = lax.axis_size("mem"), lax.axis_size("reg")
+    devices = [(m, r) for m in range(bands) for r in range(regions)]
+    pairs = [(m * regions + r, (m ^ mem) * regions + (r ^ reg)) for m, r in devices]
+    return lax.ppermute(value, ("mem", "reg"), pairs)
 
 
 def per_device(ens_state, ens_obs, innov, state_coord, obs_coord, obs_routes):
@@ -215,9 +222,9 @@
     bf16 = jnp.bfloat16
     listed = pltpu.SMEM((regions * capacity,), jnp.int32)
 
-    obs_other = swap(ens_obs, "mem", 1)
-    innov_other = swap(innov, "mem", 1)
-    state_other = swap(ens_state, "mem", 1)
+    obs_other = swap(ens_obs, mem=1)
+    innov_other = swap(innov, mem=1)
+    state_other = swap(ens_state, mem=1)
     own = (ens_obs, innov, ens_state, obs_routes.reshape(-1))
     ens_obs, innov, ens_state, routes = call(
         load_kernel,
@@ -241,9 +248,9 @@
     )
     routed, state = picked[:regions], picked[regions:]
     for step in range(1, regions):
-        routed[step] = swap(routed[step], "reg", step)
+        routed[step] = swap(routed[step], mem=1, reg=step)
     for k in range(1, chips):
-        state[k] = swap(state[k], "mem", k * CORES)
+        state[k] = swap(state[k], mem=k * CORES + 1)
     taper = call(
         functools.partial(
             taper_kernel, (regions, per_region, capacity, share, 1.0 / (members - 1))
@@ -262,7 +269,7 @@
         *routed,
     )
     for k in range(1, chips):
-        both[k] = swap(both[k], "mem", k * CORES)
+        both[k] = swap(both[k], mem=k * CORES + 1)
     increments = call(
         functools.partial(update_kernel, chips),
         [((held, rows), bf16)] * chips,
@@ -272,9 +279,9 @@
         taper,
     )
     for k in range(1, chips):
-        increments[k] = swap(increments[k], "mem", k * CORES)
+        increments[k] = swap(increments[k], mem=k * CORES + 1)
     other = call(swap_kernel, [((chips, mem_dev, rows), bf16)], [VMEM] * chips, *increments)
-    other = swap(other, "mem", 1)
+    other = swap(other, mem=1)
     return call(
         functools.partial(add_kernel, chips),
         [((mem_dev, columns), bf16)],

time: 34.2 us -> 31.7 us (0.927)
  starting transfers between devices: 18.3 us -> 16.6 us
  waiting for transfers between devices: 10.8 us -> 10.1 us
    ppermute x16, starting transfers between devices: 18.3 us -> 16.6 us  [swap(): return lax.ppermute(value, ('mem', 'reg'), pairs)]
    ppermute x16, waiting for transfers between devices: 10.8 us -> 10.1 us  [swap(): return lax.ppermute(value, ('mem', 'reg'), pairs)]
  transfers between devices with their start and end apart: 16 -> 16, of which waited for: 8 -> 9; matrix products, arithmetic and copies ran while one was open for 0% -> 0% of each run, Pallas kernels for 8% -> 9%
where the time goes in v3:
time: 31.7 us; the launch traced here: 31.6 us
  starting transfers between devices  16.6 us (52%)
  waiting for transfers between devices  10.1 us (32%)
  Pallas kernels  4.79 us (15%)
    ppermute x16, starting transfers between devices, swap(): return lax.ppermute(value, ('mem', 'reg'), pairs)  16.6 us
    ppermute x16, waiting for transfers between devices, swap(): return lax.ppermute(value, ('mem', 'reg'), pairs)  10.1 us
    pallas_call x7, Pallas kernels, call(): pl.pallas_call(kernel, out_shape=outs[0] if single else outs, in_specs=in...  4.79 us
  transfers between devices with their start and end apart: 16, of which 9 were waited for; matrix products, arithmetic and copies ran while one was open for 0% of the time, Pallas kernels for 9%

profile of v3, /device:TPU:0, one launch (start us, length us, event | category | flops | bytes accessed | tf_op | source)
XLA Modules:
  0.0 31.6 jit_solution(4247492453580535549)
XLA Ops:
  0.0 0.5 %collective-permute-start.2 = (bf16[16,4096]{1,0:T(8,128)(2,1)}, bf16[16,4096]{1,0:T(8,128)(2,1)S(1)}, u32[]{:S(2)}, u32[]{:S(2)}) collective-permute-start(bf16[16,4096]{1,0:T(8,128)(2,1)} %refs_2_.1), channel_id=1, source_target_pairs={{0,4},{1,5},{2,6},{3,7},{4,0},{5,1},{6,2},{7,3},{8,12},{9,13},{10,... | collective-permute-start | bytes 393224 | tf_op jit(solution)/shard_map/ppermute | solution.py:207
  0.5 0.5 %collective-permute-start.1 = (bf16[16,2048]{1,0:T(8,128)(2,1)}, bf16[16,2048]{1,0:T(8,128)(2,1)S(1)}, u32[]{:S(2)}, u32[]{:S(2)}) collective-permute-start(bf16[16,2048]{1,0:T(8,128)(2,1)} %refs_1_.1), channel_id=1, source_target_pairs={{0,4},{1,5},{2,6},{3,7},{4,0},{5,1},{6,2},{7,3},{8,12},{9,13},{10,... | collective-permute-start | bytes 196616 | tf_op jit(solution)/shard_map/ppermute | solution.py:207
  1.0 1.0 %shard_map.64 = (bf16[16,2048]{1,0:T(8,128)(2,1)S(1)}, bf16[16,2048]{1,0:T(8,128)(2,1)S(1)}, bf16[16,4096]{1,0:T(8,128)(2,1)S(1)}, s32[64]{0:T(128)S(1)}) custom-call(bf16[16,2048]{1,0:T(8,128)(2,1)} %refs_0_.1, bf16[16,2048]{1,0:T(8,128)(2,1)} %refs_1_.1, bf16[16,4096]{1,0:T(8,128)(2,1)} %refs_2_.1, s32[64]{0:T(128)} %bitcast.1), custom_call_target="tpu_custom_call" | custom-call | tf_op jit(solution)/shard_map/pallas_call | solution.py:192
  2.1 0.8 %shard_map.65 = (bf16[32,1024]{1,0:T(8,128)(2,1)S(1)}, bf16[32,1024]{1,0:T(8,128)(2,1)S(1)}, bf16[32,1024]{1,0:T(8,128)(2,1)S(1)}, bf16[32,1024]{1,0:T(8,128)(2,...) custom-call(s32[64]{0:T(128)S(1)} %get-tuple-element.26.routes_ref, ...), custom_call_target="tpu_custom_call" | custom-call | tf_op jit(solution)/shard_map/pallas_call | solution.py:192
  2.9 2.7 %collective-permute-start.6 = (bf16[32,1024]{1,0:T(8,128)(2,1)S(1)}, bf16[32,1024]{1,0:T(8,128)(2,1)S(1)}, u32[]{:S(2)}, u32[]{:S(2)}) collective-permute-start(bf16[32,1024]{1,0:T(8,128)(2,1)S(1)} %get-tuple-element.34), channel_id=1, source_target_pairs={{0,5},{1,4},{2,7},{3,6},{4,1},{5,0},{6,3},{7,2},{8,13},{9,12},{10,... | collective-permute-start | bytes 196616 | tf_op jit(solution)/shard_map/ppermute | solution.py:207
  5.7 2.5 %collective-permute-start.7 = (bf16[32,1024]{1,0:T(8,128)(2,1)S(1)}, bf16[32,1024]{1,0:T(8,128)(2,1)S(1)}, u32[]{:S(2)}, u32[]{:S(2)}) collective-permute-start(bf16[32,1024]{1,0:T(8,128)(2,1)S(1)} %get-tuple-element.35), channel_id=1, source_target_pairs={{0,6},{1,7},{2,4},{3,5},{4,2},{5,3},{6,0},{7,1},{8,14},{9,15},{10,... | collective-permute-start | bytes 196616 | tf_op jit(solution)/shard_map/ppermute | solution.py:207
  8.2 1.4 %collective-permute-start.3 = (bf16[32,512]{1,0:T(8,128)(2,1)S(1)}, bf16[32,512]{1,0:T(8,128)(2,1)S(1)}, u32[]{:S(2)}, u32[]{:S(2)}) collective-permute-start(bf16[32,512]{1,0:T(8,128)(2,1)S(1)} %get-tuple-element.30), channel_id=1, source_target_pairs={{0,12},{1,13},{2,14},{3,15},{4,8},{5,9},{6,10},{7,11},{8,4},{9,5},... | collective-permute-start | bytes 98312 | tf_op jit(solution)/shard_map/ppermute | solution.py:207
  9.6 1.1 %collective-permute-done.7.refs_2_ = bf16[32,1024]{1,0:T(8,128)(2,1)S(1)} collective-permute-done((bf16[32,1024]{1,0:T(8,128)(2,1)S(1)}, bf16[32,1024]{1,0:T(8,128)(2,1)S(1)}, u32[]{:S(2)}, u32[]{:S(2)}) %collective-permute-start.7) | collective-permute-done | bytes 65568 | tf_op jit(solution)/shard_map/ppermute | solution.py:207
  10.7 3.4 %collective-permute-done.8.refs_3_ = bf16[32,1024]{1,0:T(8,128)(2,1)S(1)} collective-permute-done((bf16[32,1024]{1,0:T(8,128)(2,1)S(1)}, bf16[32,1024]{1,0:T(8,128)(2,1)S(1)}, u32[]{:S(2)}, u32[]{:S(2)}) %collective-permute-start.8) | collective-permute-done | bytes 65568 | tf_op jit(solution)/shard_map/ppermute | solution.py:207
  14.3 1.3 %collective-permute-start.9 = (bf16[32,1024]{1,0:T(8,128)(2,1)S(1)}, bf16[32,1024]{1,0:T(8,128)(2,1)S(1)}, u32[]{:S(2)}, u32[]{:S(2)}) collective-permute-start(bf16[32,1024]{1,0:T(8,128)(2,1)S(1)} %get-tuple-element.38), channel_id=1, source_target_pairs={{0,12},{1,13},{2,14},{3,15},{4,8},{5,9},{6,10},{7,11},{8,4},{9,5},... | collective-permute-start | bytes 196616 | tf_op jit(solution)/shard_map/ppermute | solution.py:207
  15.6 1.5 %collective-permute-start.10 = (bf16[32,1024]{1,0:T(8,128)(2,1)S(1)}, bf16[32,1024]{1,0:T(8,128)(2,1)S(1)}, u32[]{:S(2)}, u32[]{:S(2)}) collective-permute-start(bf16[32,1024]{1,0:T(8,128)(2,1)S(1)} %get-tuple-element.39), channel_id=1, source_target_pairs={{0,20},{1,21},{2,22},{3,23},{4,16},{5,17},{6,18},{7,19},{8,28},{9,... | collective-permute-start | bytes 196616 | tf_op jit(solution)/shard_map/ppermute | solution.py:207
  17.3 1.5 %collective-permute-start.4 = (bf16[32,512]{1,0:T(8,128)(2,1)S(1)}, bf16[32,512]{1,0:T(8,128)(2,1)S(1)}, u32[]{:S(2)}, u32[]{:S(2)}) collective-permute-start(bf16[32,512]{1,0:T(8,128)(2,1)S(1)} %get-tuple-element.31), channel_id=1, source_target_pairs={{0,20},{1,21},{2,22},{3,23},{4,16},{5,17},{6,18},{7,19},{8,28},{9,... | collective-permute-start | bytes 98312 | tf_op jit(solution)/shard_map/ppermute | solution.py:207
  18.8 1.2 %collective-permute-start.5 = (bf16[32,512]{1,0:T(8,128)(2,1)S(1)}, bf16[32,512]{1,0:T(8,128)(2,1)S(1)}, u32[]{:S(2)}, u32[]{:S(2)}) collective-permute-start(bf16[32,512]{1,0:T(8,128)(2,1)S(1)} %get-tuple-element.32), channel_id=1, source_target_pairs={{0,28},{1,29},{2,30},{3,31},{4,24},{5,25},{6,26},{7,27},{8,20},{9,... | collective-permute-start | bytes 98312 | tf_op jit(solution)/shard_map/ppermute | solution.py:207
  20.0 1.7 %shard_map.67.refs_8_ = f32[512,512]{1,0:T(8,128)S(1)} custom-call(s32[64]{0:T(128)S(1)} %get-tuple-element.26.routes_ref, s32[2,4096]{1,0:T(2,128)S(1)} %copy-done.1, s32[2,8192]{1,0:T(2,128)S(1)} %copy-done), custom_call_target="tpu_custom_call" | custom-call | tf_op jit(solution)/shard_map/pallas_call | solution.py:192
  21.8 1.2 %collective-permute-done.5.refs_3_ = bf16[32,512]{1,0:T(8,128)(2,1)S(1)} collective-permute-done((bf16[32,512]{1,0:T(8,128)(2,1)S(1)}, bf16[32,512]{1,0:T(8,128)(2,1)S(1)}, u32[]{:S(2)}, u32[]{:S(2)}) %collective-permute-start.5) | collective-permute-done | bytes 32800 | tf_op jit(solution)/shard_map/ppermute | solution.py:207
  23.0 0.5 %shard_map.68 = (bf16[32,512]{1,0:T(8,128)(2,1)S(1)}, bf16[32,512]{1,0:T(8,128)(2,1)S(1)}, bf16[32,512]{1,0:T(8,128)(2,1)S(1)}, bf16[32,512]{1,0:T(8,128)(2,1)S(1)}) custom-call(bf16[32,512]{1,0:T(8,128)(2,1)S(1)} %get-tuple-element.29.refs_0_, bf16[32,512]{1,0:T(8,128)(2,1)S(1)} %collective-permute-done.3.refs_1_, ...), custom_call_target="tpu_custom_call" | custom-call | tf_op jit(solution)/shard_map/pallas_call | solution.py:192
  23.6 1.3 %collective-permute-start.12 = (bf16[32,512]{1,0:T(8,128)(2,1)S(1)}, bf16[32,512]{1,0:T(8,128)(2,1)S(1)}, u32[]{:S(2)}, u32[]{:S(2)}) collective-permute-start(bf16[32,512]{1,0:T(8,128)(2,1)S(1)} %get-tuple-element.42), channel_id=1, source_target_pairs={{0,12},{1,13},{2,14},{3,15},{4,8},{5,9},{6,10},{7,11},{8,4},{9,5},... | collective-permute-start | bytes 98312 | tf_op jit(solution)/shard_map/ppermute | solution.py:207
  24.9 0.5 %collective-permute-start.13 = (bf16[32,512]{1,0:T(8,128)(2,1)S(1)}, bf16[32,512]{1,0:T(8,128)(2,1)S(1)}, u32[]{:S(2)}, u32[]{:S(2)}) collective-permute-start(bf16[32,512]{1,0:T(8,128)(2,1)S(1)} %get-tuple-element.43), channel_id=1, source_target_pairs={{0,20},{1,21},{2,22},{3,23},{4,16},{5,17},{6,18},{7,19},{8,28},{9,... | collective-permute-start | bytes 98312 | tf_op jit(solution)/shard_map/ppermute | solution.py:207
  25.4 1.2 %collective-permute-start.14 = (bf16[32,512]{1,0:T(8,128)(2,1)S(1)}, bf16[32,512]{1,0:T(8,128)(2,1)S(1)}, u32[]{:S(2)}, u32[]{:S(2)}) collective-permute-start(bf16[32,512]{1,0:T(8,128)(2,1)S(1)} %get-tuple-element.44), channel_id=1, source_target_pairs={{0,28},{1,29},{2,30},{3,31},{4,24},{5,25},{6,26},{7,27},{8,20},{9,... | collective-permute-start | bytes 98312 | tf_op jit(solution)/shard_map/ppermute | solution.py:207
  26.6 0.4 %collective-permute-done.12.refs_1_ = bf16[32,512]{1,0:T(8,128)(2,1)S(1)} collective-permute-done((bf16[32,512]{1,0:T(8,128)(2,1)S(1)}, bf16[32,512]{1,0:T(8,128)(2,1)S(1)}, u32[]{:S(2)}, u32[]{:S(2)}) %collective-permute-start.12) | collective-permute-done | bytes 32800 | tf_op jit(solution)/shard_map/ppermute | solution.py:207
  27.0 1.2 %collective-permute-done.13.refs_2_ = bf16[32,512]{1,0:T(8,128)(2,1)S(1)} collective-permute-done((bf16[32,512]{1,0:T(8,128)(2,1)S(1)}, bf16[32,512]{1,0:T(8,128)(2,1)S(1)}, u32[]{:S(2)}, u32[]{:S(2)}) %collective-permute-start.13) | collective-permute-done | bytes 32800 | tf_op jit(solution)/shard_map/ppermute | solution.py:207
  28.2 1.4 %collective-permute-done.14.refs_3_ = bf16[32,512]{1,0:T(8,128)(2,1)S(1)} collective-permute-done((bf16[32,512]{1,0:T(8,128)(2,1)S(1)}, bf16[32,512]{1,0:T(8,128)(2,1)S(1)}, u32[]{:S(2)}, u32[]{:S(2)}) %collective-permute-start.14) | collective-permute-done | bytes 32800 | tf_op jit(solution)/shard_map/ppermute | solution.py:207
  29.8 1.1 %collective-permute-done.15.refs_4_ = bf16[4,16,512]{2,1,0:T(8,128)(2,1)S(1)} collective-permute-done((bf16[4,16,512]{2,1,0:T(8,128)(2,1)S(1)}, bf16[4,16,512]{2,1,0:T(8,128)(2,1)S(1)}, u32[]{:S(2)}, u32[]{:S(2)}) %collective-permute-start.15) | collective-permute-done | bytes 65568 | tf_op jit(solution)/shard_map/ppermute | solution.py:207
  30.9 0.7 %shard_map.70 = bf16[16,4096]{1,0:T(8,128)(2,1)} custom-call(bf16[16,4096]{1,0:T(8,128)(2,1)S(1)} %get-tuple-element.25.refs_4_.state_ref, bf16[32,512]{1,0:T(8,128)(2,1)S(1)} %get-tuple-element.41.refs_0_, bf16[32,512]{1,0:T(8,128)(2,1)S(1)} %collective-permute-done.12.refs_1_, bf16[32,512]{1,0:T(8,128)(2,1)S(1)} %collective-permute-done.13.refs_2_, ...), custom_call_target="tpu_custom_call" | custom-call | tf_op jit(solution)/shard_map/pallas_call | solution.py:192
  (19 shorter events, 0.8 us)
Async XLA Ops:
  0.0 2.1 %collective-permute-start.2 = (bf16[16,4096]{1,0:T(8,128)(2,1)}, bf16[16,4096]{1,0:T(8,128)(2,1)S(1)}, u32[]{:S(2)}, u32[]{:S(2)}) collective-permute-start(bf16[16,4096]{1,0:T(8,128)(2,1)} %refs_2_.1), channel_id=1, source_target_pairs={{0,4},{1,5},{2,6},{3,7},{4,0},{5,1},{6,2},{7,3},{8,12},{9,13},{10,... | collective-permute-start | bytes 393224 | tf_op jit(solution)/shard_map/ppermute | solution.py:207
  0.5 1.5 %collective-permute-start = (bf16[16,2048]{1,0:T(8,128)(2,1)}, bf16[16,2048]{1,0:T(8,128)(2,1)S(1)}, u32[]{:S(2)}, u32[]{:S(2)}) collective-permute-start(bf16[16,2048]{1,0:T(8,128)(2,1)} %refs_0_.1), channel_id=1, source_target_pairs={{0,4},{1,5},{2,6},{3,7},{4,0},{5,1},{6,2},{7,3},{8,12},{9,13},{10,... | collective-permute-start | bytes 196616 | tf_op jit(solution)/shard_map/ppermute | solution.py:207
  0.5 1.6 %collective-permute-start.1 = (bf16[16,2048]{1,0:T(8,128)(2,1)}, bf16[16,2048]{1,0:T(8,128)(2,1)S(1)}, u32[]{:S(2)}, u32[]{:S(2)}) collective-permute-start(bf16[16,2048]{1,0:T(8,128)(2,1)} %refs_1_.1), channel_id=1, source_target_pairs={{0,4},{1,5},{2,6},{3,7},{4,0},{5,1},{6,2},{7,3},{8,12},{9,13},{10,... | collective-permute-start | bytes 196616 | tf_op jit(solution)/shard_map/ppermute | solution.py:207
  2.9 6.7 %collective-permute-start.6 = (bf16[32,1024]{1,0:T(8,128)(2,1)S(1)}, bf16[32,1024]{1,0:T(8,128)(2,1)S(1)}, u32[]{:S(2)}, u32[]{:S(2)}) collective-permute-start(bf16[32,1024]{1,0:T(8,128)(2,1)S(1)} %get-tuple-element.34), channel_id=1, source_target_pairs={{0,5},{1,4},{2,7},{3,6},{4,1},{5,0},{6,3},{7,2},{8,13},{9,12},{10,... | collective-permute-start | bytes 196616 | tf_op jit(solution)/shard_map/ppermute | solution.py:207
  5.7 5.1 %collective-permute-start.7 = (bf16[32,1024]{1,0:T(8,128)(2,1)S(1)}, bf16[32,1024]{1,0:T(8,128)(2,1)S(1)}, u32[]{:S(2)}, u32[]{:S(2)}) collective-permute-start(bf16[32,1024]{1,0:T(8,128)(2,1)S(1)} %get-tuple-element.35), channel_id=1, source_target_pairs={{0,6},{1,7},{2,4},{3,5},{4,2},{5,3},{6,0},{7,1},{8,14},{9,15},{10,... | collective-permute-start | bytes 196616 | tf_op jit(solution)/shard_map/ppermute | solution.py:207
  8.2 6.0 %collective-permute-start.8 = (bf16[32,1024]{1,0:T(8,128)(2,1)S(1)}, bf16[32,1024]{1,0:T(8,128)(2,1)S(1)}, u32[]{:S(2)}, u32[]{:S(2)}) collective-permute-start(bf16[32,1024]{1,0:T(8,128)(2,1)S(1)} %get-tuple-element.36), channel_id=1, source_target_pairs={{0,7},{1,6},{2,5},{3,4},{4,3},{5,2},{6,1},{7,0},{8,15},{9,14},{10,... | collective-permute-start | bytes 196616 | tf_op jit(solution)/shard_map/ppermute | solution.py:207
  8.2 10.5 %collective-permute-start.3 = (bf16[32,512]{1,0:T(8,128)(2,1)S(1)}, bf16[32,512]{1,0:T(8,128)(2,1)S(1)}, u32[]{:S(2)}, u32[]{:S(2)}) collective-permute-start(bf16[32,512]{1,0:T(8,128)(2,1)S(1)} %get-tuple-element.30), channel_id=1, source_target_pairs={{0,12},{1,13},{2,14},{3,15},{4,8},{5,9},{6,10},{7,11},{8,4},{9,5},... | collective-permute-start | bytes 98312 | tf_op jit(solution)/shard_map/ppermute | solution.py:207
  14.2 5.8 %copy-start = (s32[2,8192]{1,0:T(2,128)S(1)}, s32[2,8192]{1,0:T(2,128)}, u32[]{:S(2)}) copy-start(s32[2,8192]{1,0:T(2,128)} %obs_ref.1) | copy-start | bytes 196612
  14.2 5.8 %copy-start.1 = (s32[2,4096]{1,0:T(2,128)S(1)}, s32[2,4096]{1,0:T(2,128)}, u32[]{:S(2)}) copy-start(s32[2,4096]{1,0:T(2,128)} %rows_ref.1) | copy-start | bytes 98308
  14.3 8.8 %collective-permute-start.9 = (bf16[32,1024]{1,0:T(8,128)(2,1)S(1)}, bf16[32,1024]{1,0:T(8,128)(2,1)S(1)}, u32[]{:S(2)}, u32[]{:S(2)}) collective-permute-start(bf16[32,1024]{1,0:T(8,128)(2,1)S(1)} %get-tuple-element.38), channel_id=1, source_target_pairs={{0,12},{1,13},{2,14},{3,15},{4,8},{5,9},{6,10},{7,11},{8,4},{9,5},... | collective-permute-start | bytes 196616 | tf_op jit(solution)/shard_map/ppermute | solution.py:207
  15.6 7.4 %collective-permute-start.10 = (bf16[32,1024]{1,0:T(8,128)(2,1)S(1)}, bf16[32,1024]{1,0:T(8,128)(2,1)S(1)}, u32[]{:S(2)}, u32[]{:S(2)}) collective-permute-start(bf16[32,1024]{1,0:T(8,128)(2,1)S(1)} %get-tuple-element.39), channel_id=1, source_target_pairs={{0,20},{1,21},{2,22},{3,23},{4,16},{5,17},{6,18},{7,19},{8,28},{9,... | collective-permute-start | bytes 196616 | tf_op jit(solution)/shard_map/ppermute | solution.py:207
  17.0 6.0 %collective-permute-start.11 = (bf16[32,1024]{1,0:T(8,128)(2,1)S(1)}, bf16[32,1024]{1,0:T(8,128)(2,1)S(1)}, u32[]{:S(2)}, u32[]{:S(2)}) collective-permute-start(bf16[32,1024]{1,0:T(8,128)(2,1)S(1)} %get-tuple-element.40), channel_id=1, source_target_pairs={{0,28},{1,29},{2,30},{3,31},{4,24},{5,25},{6,26},{7,27},{8,20},{9,... | collective-permute-start | bytes 196616 | tf_op jit(solution)/shard_map/ppermute | solution.py:207
  17.3 4.5 %collective-permute-start.4 = (bf16[32,512]{1,0:T(8,128)(2,1)S(1)}, bf16[32,512]{1,0:T(8,128)(2,1)S(1)}, u32[]{:S(2)}, u32[]{:S(2)}) collective-permute-start(bf16[32,512]{1,0:T(8,128)(2,1)S(1)} %get-tuple-element.31), channel_id=1, source_target_pairs={{0,20},{1,21},{2,22},{3,23},{4,16},{5,17},{6,18},{7,19},{8,28},{9,... | collective-permute-start | bytes 98312 | tf_op jit(solution)/shard_map/ppermute | solution.py:207
  18.8 4.2 %collective-permute-start.5 = (bf16[32,512]{1,0:T(8,128)(2,1)S(1)}, bf16[32,512]{1,0:T(8,128)(2,1)S(1)}, u32[]{:S(2)}, u32[]{:S(2)}) collective-permute-start(bf16[32,512]{1,0:T(8,128)(2,1)S(1)} %get-tuple-element.32), channel_id=1, source_target_pairs={{0,28},{1,29},{2,30},{3,31},{4,24},{5,25},{6,26},{7,27},{8,20},{9,... | collective-permute-start | bytes 98312 | tf_op jit(solution)/shard_map/ppermute | solution.py:207
  23.6 3.4 %collective-permute-start.12 = (bf16[32,512]{1,0:T(8,128)(2,1)S(1)}, bf16[32,512]{1,0:T(8,128)(2,1)S(1)}, u32[]{:S(2)}, u32[]{:S(2)}) collective-permute-start(bf16[32,512]{1,0:T(8,128)(2,1)S(1)} %get-tuple-element.42), channel_id=1, source_target_pairs={{0,12},{1,13},{2,14},{3,15},{4,8},{5,9},{6,10},{7,11},{8,4},{9,5},... | collective-permute-start | bytes 98312 | tf_op jit(solution)/shard_map/ppermute | solution.py:207
  24.9 3.3 %collective-permute-start.13 = (bf16[32,512]{1,0:T(8,128)(2,1)S(1)}, bf16[32,512]{1,0:T(8,128)(2,1)S(1)}, u32[]{:S(2)}, u32[]{:S(2)}) collective-permute-start(bf16[32,512]{1,0:T(8,128)(2,1)S(1)} %get-tuple-element.43), channel_id=1, source_target_pairs={{0,20},{1,21},{2,22},{3,23},{4,16},{5,17},{6,18},{7,19},{8,28},{9,... | collective-permute-start | bytes 98312 | tf_op jit(solution)/shard_map/ppermute | solution.py:207
  25.4 4.2 %collective-permute-start.14 = (bf16[32,512]{1,0:T(8,128)(2,1)S(1)}, bf16[32,512]{1,0:T(8,128)(2,1)S(1)}, u32[]{:S(2)}, u32[]{:S(2)}) collective-permute-start(bf16[32,512]{1,0:T(8,128)(2,1)S(1)} %get-tuple-element.44), channel_id=1, source_target_pairs={{0,28},{1,29},{2,30},{3,31},{4,24},{5,25},{6,26},{7,27},{8,20},{9,... | collective-permute-start | bytes 98312 | tf_op jit(solution)/shard_map/ppermute | solution.py:207
  29.6 1.3 %collective-permute-start.15 = (bf16[4,16,512]{2,1,0:T(8,128)(2,1)S(1)}, bf16[4,16,512]{2,1,0:T(8,128)(2,1)S(1)}, u32[]{:S(2)}, u32[]{:S(2)}) collective-permute-start(bf16[4,16,512]{2,1,0:T(8,128)(2,1)S(1)} %shard_map.69), channel_id=1, source_target_pairs={{0,4},{1,5},{2,6},{3,7},{4,0},{5,1},{6,2},{7,3},{8,12},{9,13},{10,... | collective-permute-start | bytes 196616 | tf_op jit(solution)/shard_map/ppermute | solution.py:207
